TPU v7x, 256 devices: a whole 4x4x8 slice. The times are simulated.
256 devices in a mesh: grp: 4 (over x), shard: 64 (over z, y, core).
Axes of the slice: x: 4, y: 4, z: 8, core: 2. Of those that a mesh axis runs over, the one named last changes fastest.
Arguments:
- cells: bfloat16 [1024, 64, 768], P('shard'), may hold values from -8 to 8
- w_cell: bfloat16 [768, 768], replicated, may hold values from -0.21875 to 0.21875
- w_mix: bfloat16 [768, 768], replicated, may hold values from -0.21875 to 0.21875
- w_pool: bfloat16 [768, 768], replicated, may hold values from -0.21875 to 0.21875
- pairs: int32 [16384, 2], P(('grp', 'shard')), may hold values from 0 to 1023, as said below
- counts: int32 [256], P(('grp', 'shard')), may hold values from 1 to 64, 12288 in all
Outputs:
- scores: float32 [16384], P(('grp', 'shard'))
Inputs may be any that keep to these rules, and one draw needn't show every extreme that they name: Column c lies on shard index c // 16. The first column of each pair of reader r lies on shard index r % 64. Among the 64 pairs of one reader at most 2 have their second column on one shard index, and on some shard index exactly 2. The two columns of a pair differ.
All inputs are finite; a program needn't handle non-finite values. No bound on the sum of `counts` on one device may be relied on, other than what follows from the above.
Results may differ from a plain program's by a relative error of at most 0.0014.
Values may be sent and summed in bfloat16 or wider, within the bound.
A program may use at most 192 MiB of HBM per device.

v0:
```python
import math

import jax
import jax.numpy as jnp
from jax import lax
from jax.sharding import PartitionSpec as P

SOFTMAX_WARMTH = 0.07
EPSILON = 1e-06


def pair_scores(left_block, right_block, w_mix, w_pool):
    score_scale = 1.0 / math.sqrt(left_block.shape[2])
    forward = (
        jnp.einsum("psd,ptd->pst", left_block, right_block, preferred_element_type=jnp.float32)
        * score_scale
    )
    backward = (
        jnp.einsum("ptd,psd->pts", right_block, left_block, preferred_element_type=jnp.float32)
        * score_scale
    )
    attend_left_side = jax.nn.softmax(forward, axis=-1).astype(jnp.bfloat16)
    attend_right = jax.nn.softmax(backward, axis=-1).astype(jnp.bfloat16)
    context_left = jnp.einsum(
        "pst,ptd->psd", attend_left_side, right_block, preferred_element_type=jnp.float32
    )
    context_right = jnp.einsum(
        "pts,psd->ptd", attend_right, left_block, preferred_element_type=jnp.float32
    )
    mixed_left = (left_block.astype(jnp.float32) + context_left).astype(jnp.bfloat16)
    mixed_right = (right_block.astype(jnp.float32) + context_right).astype(jnp.bfloat16)
    pooled_left = jnp.mean(
        jnp.tanh(jnp.einsum("psd,de->pse", mixed_left, w_mix, preferred_element_type=jnp.float32)),
        axis=1,
    ).astype(jnp.bfloat16)
    pooled_right = jnp.mean(
        jnp.tanh(jnp.einsum("psd,de->pse", mixed_right, w_mix, preferred_element_type=jnp.float32)),
        axis=1,
    ).astype(jnp.bfloat16)
    z_left = jnp.dot(pooled_left, w_pool, preferred_element_type=jnp.float32)
    z_right = jnp.dot(pooled_right, w_pool, preferred_element_type=jnp.float32)
    inner_product = jnp.mean(z_left * z_right, axis=-1)
    vector_norms = (jnp.mean(z_left * z_left, axis=-1) + EPSILON) * (
        jnp.mean(z_right * z_right, axis=-1) + EPSILON
    )
    return inner_product / jnp.sqrt(vector_norms) / SOFTMAX_WARMTH


def local(cells, w_cell, w_mix, w_pool, pairs, counts):
    col_dev, samples, features = cells.shape
    shards = lax.axis_size("shard")
    pair_dev = pairs.shape[0]
    bucket_capacity = 2 * pair_dev // shards
    projected = jnp.dot(
        cells.reshape(col_dev * samples, features), w_cell, preferred_element_type=jnp.float32
    )
    projected = projected.astype(jnp.bfloat16).reshape(col_dev, samples, features)
    left_local = pairs[:, 0] % col_dev
    right_ids = pairs[:, 1]
    owners = right_ids // col_dev
    right_local = right_ids % col_dev
    position_index = jnp.arange(pair_dev, dtype=jnp.int32)
    same_owner = owners[:, None] == owners[None, :]
    earlier = position_index[None, :] < position_index[:, None]
    ranks = jnp.sum(jnp.where(same_owner & earlier, 1, 0), axis=1).astype(jnp.int32)
    slots = owners * bucket_capacity + ranks
    live_count = counts[0]
    bucket_ids = jnp.arange(shards * bucket_capacity, dtype=jnp.int32)
    slot_match = slots[:, None] == bucket_ids[None, :]
    requests = jnp.sum(jnp.where(slot_match, right_local[:, None], 0), axis=0)
    requests = requests.reshape(shards, bucket_capacity)
    asked = lax.all_to_all(requests, "shard", split_axis=0, concat_axis=0, tiled=True)
    found = jnp.take(projected, asked.reshape(-1), axis=0)
    found = found.reshape(asked.shape[0], asked.shape[1], samples, features)
    fetched = lax.all_to_all(found, "shard", split_axis=0, concat_axis=0, tiled=True)
    right_blocks = jnp.take(
        fetched.reshape(shards * bucket_capacity, samples, features), slots, axis=0
    )

    def score_block(block_index, totals):
        first = block_index * 8
        left_sel = lax.dynamic_slice_in_dim(left_local, first, 8, 0)
        left_block = jnp.take(projected, left_sel, axis=0)
        right_block = lax.dynamic_slice_in_dim(right_blocks, first, 8, 0)
        value_rows = pair_scores(left_block, right_block, w_mix, w_pool)
        return lax.dynamic_update_slice_in_dim(totals, value_rows, first, 0)

    block_total = (live_count + 7) // 8
    value_rows = lax.fori_loop(0, block_total, score_block, jnp.zeros((pair_dev,), jnp.float32))
    return jnp.where(position_index < live_count, value_rows, jnp.zeros_like(value_rows))


def solution(mesh):
    placed = (P("shard", None, None), P(), P(), P(), P(("grp", "shard"), None), P(("grp", "shard")))
    return jax.shard_map(
        local, mesh=mesh, in_specs=placed, out_specs=P(("grp", "shard")), check_vma=False
    )
```

profile of v0, /device:TPU:1, one launch (start us, length us, event | category | flops | bytes accessed | tf_op | source)
XLA Modules:
  0.0 456.6 jit_solution(13180424467836346009)
XLA Ops:
  2.6 13.1 %all-to-all-start = ((s32[64,1,2]{2,1,0:T(1,128)}), s32[64,1,2]{2,1,0:T(1,128)S(1)}, u32[]{:S(2)}, u32[]{:S(2)}) async-start(s32[64,1,2]{2,1,0:T(1,128)} %bitcast.11), calls=%async_computation | async-start | bytes 65536 | tf_op jit(solution)/shard_map/all_to_all | solution.py:72
  15.8 2.7 convolution_convert_fusion
  18.4 6.7 %all-to-all-done = s32[64,1,2]{2,1,0:T(1,128)S(1)} async-done(((s32[64,1,2]{2,1,0:T(1,128)}), s32[64,1,2]{2,1,0:T(1,128)S(1)}, u32[]{:S(2)}, u32[]{:S(2)}) %all-to-all-start) | async-done | bytes 544 | tf_op jit(solution)/shard_map/all_to_all | solution.py:72
  26.8 8.3 %gather_fusion.1 = bf16[128,64,768]{2,1,0:T(8,128)(2,1)} fusion(bf16[16,64,768]{2,1,0:T(8,128)(2,1)S(1)} %bitcast.69, s32[1024]{0:T(1024)S(1)} %pad_clamp_fusion.2), kind=kCustom, calls=%fused_computation.1 | custom fusion | bytes 25166336 | tf_op jit(solution)/shard_map/jit(_take)/gather | solution.py:73
  35.1 10.8 %broadcast_select_fusion.6 = bf16[64,2,64,768]{3,2,1,0:T(8,128)(2,1)} fusion(bf16[64,2,64,768]{3,2,1,0:T(8,128)(2,1)} %bitcast.71, pred[64,2]{1,0:T(8,128)(4,1)S(1)} %copy.20), kind=kLoop, calls=%fused_computation.47 | loop fusion | flops 6291456 | bytes 25165952 | tf_op jit(solution)/shard_map/jit(_take)/select_n | solution.py:73
  45.9 5.8 %all-to-all-start.1 = ((bf16[64,2,64,768]{3,2,1,0:T(8,128)(2,1)}), bf16[64,2,64,768]{3,2,1,0:T(8,128)(2,1)}, u32[]{:S(2)}, u32[]{:S(2)}) async-start(bf16[64,2,64,768]{3,2,1,0:T(8,128)(2,1)} %broadcast_select_fusion.6), calls=%async_computation.1 | async-start | bytes 25165824 | tf_op jit(solution)/shard_map/all_to_all | solution.py:75
  52.4 273.9 %all-to-all-done.1 = bf16[64,2,64,768]{3,2,1,0:T(8,128)(2,1)} async-done(((bf16[64,2,64,768]{3,2,1,0:T(8,128)(2,1)}), bf16[64,2,64,768]{3,2,1,0:T(8,128)(2,1)}, u32[]{:S(2)}, u32[]{:S(2)}) %all-to-all-start.1) | async-done | bytes 12582944 | tf_op jit(solution)/shard_map/all_to_all | solution.py:75
  326.3 8.1 %gather_fusion.2 = bf16[64,64,768]{2,1,0:T(8,128)(2,1)} fusion(bf16[128,64,768]{2,1,0:T(8,128)(2,1)} %bitcast.15, s32[1024]{0:T(1024)S(1)} %pad_clamp_fusion.1), kind=kCustom, calls=%fused_computation.2 | custom fusion | bytes 12583168 | tf_op jit(solution)/shard_map/jit(_take)/gather | solution.py:76
  334.4 6.1 %broadcast_select_fusion.7 = bf16[64,64,768]{2,1,0:T(8,128)(2,1)} fusion(bf16[64,64,768]{2,1,0:T(8,128)(2,1)} %gather_fusion.2, pred[64]{0:T(512)(128)(4,1)S(1)} %and_bitcast_fusion), kind=kLoop, calls=%fused_computation.48 | loop fusion | flops 3145728 | bytes 12582976 | tf_op jit(solution)/shard_map/jit(_take)/select_n | solution.py:76
  340.5 115.6 %while.10 = (s32[]{:T(128)}, f32[64]{0:T(128)S(1)}, s32[]{:T(128)}, s32[64]{0:T(128)S(1)}, bf16[16,64,768]{2,1,0:T(8,128)(2,1)S(1)}, /*index=5*/bf16[64,64,768]{...) while((s32[]{:T(128)}, f32[64]{0:T(128)S(1)}, s32[]{:T(128)}, ...), condition=%wide.region_12.13_spmd, body=%wide.region_2.12_spmd.sunk | while | flops 1433323776 | bytes 14322867 | solution.py:89
  343.9 2.9 tanh_reduce_fusion.5
  348.7 2.9 tanh_reduce_fusion.4
  356.5 1.8 convolution_multiply_fusion.5
  358.4 2.9 tanh_reduce_fusion.5
  363.2 2.9 tanh_reduce_fusion.4
  370.9 1.8 convolution_multiply_fusion.5
  372.8 2.9 tanh_reduce_fusion.5
  377.6 2.9 tanh_reduce_fusion.4
  385.4 1.8 convolution_multiply_fusion.5
  387.3 2.9 tanh_reduce_fusion.5
  392.1 2.9 tanh_reduce_fusion.4
  399.8 1.8 convolution_multiply_fusion.5
  401.7 2.9 tanh_reduce_fusion.5
  406.5 2.9 tanh_reduce_fusion.4
  414.3 1.8 convolution_multiply_fusion.5
  416.2 2.9 tanh_reduce_fusion.5
  421.0 2.9 tanh_reduce_fusion.4
  430.6 2.9 tanh_reduce_fusion.5
  435.4 2.9 tanh_reduce_fusion.4
  443.2 1.8 convolution_multiply_fusion.5
  445.1 2.9 tanh_reduce_fusion.5
  449.9 2.9 tanh_reduce_fusion.4
  (94 shorter events, 63.3 us)
Async XLA Ops:
  0.0 15.8 %copy-start = (bf16[16,64,768]{2,1,0:T(8,128)(2,1)S(1)}, bf16[16,64,768]{2,1,0:T(8,128)(2,1)}, u32[]{:S(2)}) copy-start(bf16[16,64,768]{2,1,0:T(8,128)(2,1)} %param.8) | copy-start | bytes 4718596
  2.6 22.6 %all-to-all-start = ((s32[64,1,2]{2,1,0:T(1,128)}), s32[64,1,2]{2,1,0:T(1,128)S(1)}, u32[]{:S(2)}, u32[]{:S(2)}) async-start(s32[64,1,2]{2,1,0:T(1,128)} %bitcast.11), calls=%async_computation | async-start | bytes 65536 | tf_op jit(solution)/shard_map/all_to_all | solution.py:72
  45.9 280.4 %all-to-all-start.1 = ((bf16[64,2,64,768]{3,2,1,0:T(8,128)(2,1)}), bf16[64,2,64,768]{3,2,1,0:T(8,128)(2,1)}, u32[]{:S(2)}, u32[]{:S(2)}) async-start(bf16[64,2,64,768]{3,2,1,0:T(8,128)(2,1)} %broadcast_select_fusion.6), calls=%async_computation.1 | async-start | bytes 25165824 | tf_op jit(solution)/shard_map/all_to_all | solution.py:75
where the time goes:
time: 461 us; the launch traced here: 457 us
  waiting for transfers between devices  281 us (61%)
  matrix products  103 us (22%)
  local copies, waits for them, and re-layouts  29.8 us (6%)
  other arithmetic  22.9 us (5%)
  starting transfers between devices  18.9 us (4%)
    all_to_all x1, waiting for transfers between devices, local(): lax.all_to_all(found, 'shard', split_axis=0, concat_axis=0, tiled=True)  274 us
    dot_general x8, matrix products, pair_scores(): jnp.einsum('psd,de->pse', mixed_left, w_mix, preferred_element_type=jnp.f...  23 us
    dot_general x8, matrix products, pair_scores(): jnp.einsum('psd,de->pse', mixed_right, w_mix, preferred_element_type=jnp....  22.9 us
    dot_general x8, matrix products, pair_scores(): jnp.einsum('psd,ptd->pst', left_block, right_block, preferred_element_typ...  14.4 us
    dot_general x8, matrix products, pair_scores(): jnp.einsum('ptd,psd->pts', right_block, left_block, preferred_element_typ...  14.3 us
    dot_general x8, matrix products, pair_scores(): z_left = jnp.dot(pooled_left, w_pool, preferred_element_type=jnp.float32)  13.7 us
    all_to_all x1, starting transfers between devices, local(): lax.all_to_all(requests, 'shard', split_axis=0, concat_axis=0, tiled=True)  13.1 us
    dot_general x8, matrix products, pair_scores(): z_right = jnp.dot(pooled_right, w_pool, preferred_element_type=jnp.float32)  12.3 us
  transfers between devices with their start and end apart: 2, of which 2 were waited for; matrix products, arithmetic and copies ran while one was open for 1% of the time, Pallas kernels for 0%

commit v1 on v0

v1 whole, which is shorter than its diff:
```python
import functools
import math

import jax
import jax.numpy as jnp
from jax import lax
from jax.experimental import pallas as pl
from jax.experimental.pallas import tpu as pltpu
from jax.sharding import PartitionSpec as P

SOFTMAX_WARMTH = 0.07
EPSILON = 1e-06
MESH = pl.DeviceIdType.MESH
CAPACITY = 512
GROUP = 4


def place():
    x = lax.axis_index("grp")
    shard = lax.axis_index("shard")
    return x, lax.rem(shard // 2, 4), shard // 8, lax.rem(shard, 2)


def gather_kernel(proj, code, sa, sb, plist, stage, send_sem, recv_sem, local_sem):
    x, y, z, core = place()
    shard = lambda z_, y_, c_: z_ * 8 + y_ * 2 + c_
    xr, xl = lax.rem(x + 1, 4), lax.rem(x + 3, 4)
    yr, yl, yo = lax.rem(y + 1, 4), lax.rem(y + 3, 4), lax.rem(y + 2, 4)
    zs = [lax.rem(z + k, 8) for k in range(8)]
    me = shard(z, y, core)
    dev = {
        "x+": (xr, me),
        "x-": (xl, me),
        "y+": (x, shard(z, yr, core)),
        "y-": (x, shard(z, yl, core)),
        "z+": (x, shard(zs[1], y, core)),
        "z-": (x, shard(zs[7], y, core)),
        "c": (x, shard(z, y, 1 - core)),
    }
    barrier = pltpu.get_barrier_semaphore()
    for d in dev.values():
        pl.semaphore_signal(barrier, inc=1, device_id=d, device_id_type=MESH)

    fetch = pltpu.make_async_copy(proj, stage, local_sem.at[0])
    fetch.start()
    fetch.wait()
    pl.semaphore_wait(barrier, len(dev))

    kinds = {}
    sent = []

    def index_of(kind):
        return kinds.setdefault(kind, len(kinds))

    def send(kind, src, dst, to):
        k = index_of(kind)
        copy = pltpu.make_async_remote_copy(
            src_ref=src, dst_ref=dst, send_sem=send_sem.at[k], recv_sem=recv_sem.at[k],
            device_id=dev[to], device_id_type=MESH,
        )
        copy.start()
        sent.append(copy)

    def arrive(kind, slot, to):
        k = index_of(kind)
        pltpu.make_async_remote_copy(
            src_ref=slot, dst_ref=slot, send_sem=send_sem.at[k], recv_sem=recv_sem.at[k],
            device_id=dev[to], device_id_type=MESH,
        ).wait_recv()

    def a_cols(y_, first, size):
        return sa.at[pl.ds(y_ * 16 + first, size)]

    def b_cols(z_, c_, first, size):
        return sb.at[pl.ds(z_ * 8 + c_ * 4 + first, size)]

    keep = [
        pltpu.make_async_copy(stage, a_cols(y, 0, 16), local_sem.at[1]),
        pltpu.make_async_copy(stage.at[pl.ds(4 * x, 4)], b_cols(z, core, 0, 4), local_sem.at[2]),
        pltpu.make_async_copy(code, plist.at[x, y], local_sem.at[3]),
    ]
    send("l+", code, plist.at[x, y], "y+")
    send("l-", code, plist.at[x, y], "y-")
    for p in (0, 1):
        send(f"z+0{p}", stage.at[pl.ds(4 * x + 2 * p, 2)], b_cols(z, core, 2 * p, 2), "z+")
        send(f"z-0{p}", stage.at[pl.ds(4 * x + 2 * (1 - p), 2)], b_cols(z, core, 2 * (1 - p), 2), "z-")
    send("y+S", stage.at[pl.ds(2 * x, 2)], a_cols(y, 2 * x, 2), "y+")
    send("y-S", stage.at[pl.ds(2 * x, 2)], a_cols(y, 2 * x, 2), "y-")
    send("y+D0", stage.at[pl.ds(8, 3)], a_cols(y, 8, 3), "y+")
    send("y-D1", stage.at[pl.ds(11, 5)], a_cols(y, 11, 5), "y-")
    send("c0", stage.at[pl.ds(4 * x, 4)], b_cols(z, core, 0, 4), "c")
    for copy in keep:
        copy.start()

    def z_round(d, p):
        up = b_cols(zs[8 - d], core, 2 * p, 2)
        down = b_cols(zs[d], core, 2 * (1 - p), 2)
        arrive(f"z+{d - 1}{p}", up, "z-")
        if d < 3 or (d == 3 and p == 0):
            send(f"z+{d}{p}", up, up, "z+")
        send(f"c+{d}{p}", up, up, "c")
        arrive(f"z-{d - 1}{p}", down, "z+")
        if d < 3 or (d == 3 and p == 0):
            send(f"z-{d}{p}", down, down, "z-")
        send(f"c-{d}{p}", down, down, "c")

    arrive("l+", plist.at[x, yl], "y-")
    send("l+2", plist.at[x, yl], plist.at[x, yl], "y+")
    arrive("l-", plist.at[x, yr], "y+")

    below, above, far = a_cols(yl, 2 * x, 2), a_cols(yr, 2 * x, 2), a_cols(yo, 2 * x, 2)
    arrive("y+S", below, "y-")
    send("y+S2", below, below, "y+")
    send("x+b", below, below, "x+")
    send("x-b", below, below, "x-")
    arrive("y-S", above, "y+")
    send("x+a", above, above, "x+")
    send("x-a", above, above, "x-")
    send("y+D1", stage.at[pl.ds(11, 5)], a_cols(y, 11, 5), "y+")
    send("y-D0", stage.at[pl.ds(8, 3)], a_cols(y, 8, 3), "y-")
    z_round(1, 0)

    arrive("l+2", plist.at[x, yo], "y-")
    keep[2].wait()
    send("lx+", plist.at[x], plist.at[x], "x+")
    send("lx-", plist.at[x], plist.at[x], "x-")
    z_round(1, 1)

    arrive("y+D0", a_cols(yl, 8, 3), "y-")
    send("y+D02", a_cols(yl, 8, 3), a_cols(yl, 8, 3), "y+")
    got = a_cols(yl, 2 * xl, 2)
    arrive("x+b", got, "x-")
    send("x+b2", got, got, "x+")
    z_round(2, 0)

    arrive("lx+", plist.at[xl], "x-")
    send("lx+2", plist.at[xl], plist.at[xl], "x+")
    got = a_cols(yr, 2 * xr, 2)
    arrive("x-a", got, "x+")
    send("x-a2", got, got, "x-")
    arrive("y-D1", a_cols(yr, 11, 5), "y+")
    send("y-D12", a_cols(yr, 11, 5), a_cols(yr, 11, 5), "y-")
    arrive("y+S2", far, "y-")
    for j in (0, 1):
        one = a_cols(yo, 2 * x + j, 1)
        send(f"x+f{j}", one, one, "x+")
        send(f"x-f{1 - j}", a_cols(yo, 2 * x + 1 - j, 1), a_cols(yo, 2 * x + 1 - j, 1), "x-")
    z_round(2, 1)
    z_round(3, 0)
    got = a_cols(yo, 2 * xl, 1)
    arrive("x+f0", got, "x-")
    send("x+f02", got, got, "x+")
    got = a_cols(yo, 2 * xr + 1, 1)
    arrive("x-f1", got, "x+")
    send("x-f12", got, got, "x-")
    z_round(3, 1)
    z_round(4, 0)

    xo = lax.rem(x + 2, 4)
    arrive("y-D0", a_cols(yr, 8, 3), "y+")
    arrive("y+D1", a_cols(yl, 11, 5), "y-")
    arrive("y+D02", a_cols(yo, 8, 3), "y-")
    arrive("y-D12", a_cols(yo, 11, 5), "y+")
    arrive("x-b", a_cols(yl, 2 * xr, 2), "x+")
    arrive("x+a", a_cols(yr, 2 * xl, 2), "x-")
    arrive("x+b2", a_cols(yl, 2 * xo, 2), "x-")
    arrive("x-a2", a_cols(yr, 2 * xo, 2), "x+")
    arrive("x+f1", a_cols(yo, 2 * xl + 1, 1), "x-")
    arrive("x-f0", a_cols(yo, 2 * xr, 1), "x+")
    arrive("x+f02", a_cols(yo, 2 * xo, 1), "x-")
    arrive("x-f12", a_cols(yo, 2 * xo + 1, 1), "x+")
    arrive("lx-", plist.at[xr], "x+")
    arrive("lx+2", plist.at[xo], "x-")
    other = 1 - core
    arrive("c0", b_cols(z, other, 0, 4), "c")
    for d, p in ((1, 0), (1, 1), (2, 0), (2, 1), (3, 0), (3, 1), (4, 0)):
        arrive(f"c+{d}{p}", b_cols(zs[8 - d], other, 2 * p, 2), "c")
        arrive(f"c-{d}{p}", b_cols(zs[d], other, 2 * (1 - p), 2), "c")
    keep[0].wait()
    keep[1].wait()
    for copy in sent:
        copy.wait_send()
    assert len(kinds) <= COPIES and len(kinds) == len(sent)


COPIES = 80


def gather_blocks(projected, code):
    any_space = pl.BlockSpec(memory_space=pl.ANY)
    columns, samples, features = projected.shape
    return pl.pallas_call(
        gather_kernel,
        out_shape=(
            jax.ShapeDtypeStruct((64, samples, features), jnp.bfloat16),
            jax.ShapeDtypeStruct((64, samples, features), jnp.bfloat16),
            jax.ShapeDtypeStruct((4, 4, 1, 128), jnp.int32),
        ),
        in_specs=[any_space, any_space],
        out_specs=(any_space, any_space, any_space),
        scratch_shapes=[
            pltpu.VMEM((columns, samples, features), jnp.bfloat16),
            pltpu.SemaphoreType.DMA((COPIES,)),
            pltpu.SemaphoreType.DMA((COPIES,)),
            pltpu.SemaphoreType.DMA((4,)),
        ],
        compiler_params=pltpu.CompilerParams(collective_id=0, has_side_effects=True),
        name="gather_blocks",
    )(projected, code)


def score_kernel(
    lst, target, w_mix, w_pool, sa, sb, out, a_buf, b_buf, mixed, pooled, acc, sem
):
    features = w_mix.shape[0]
    samples = a_buf.shape[2]
    scale = 1.0 / math.sqrt(features)
    count = lst[CAPACITY]
    steps = (count + GROUP - 1) // GROUP

    def copies(step, slot):
        found = []
        for j in range(GROUP):
            entry = lst[step * GROUP + j]
            found.append(
                pltpu.make_async_copy(sa.at[entry & 63], a_buf.at[slot, j], sem.at[slot, 0, j])
            )
            found.append(
                pltpu.make_async_copy(sb.at[entry >> 6], b_buf.at[slot, j], sem.at[slot, 1, j])
            )
        return found

    acc[...] = jnp.zeros_like(acc)

    @pl.when(steps > 0)
    def _():
        for copy in copies(0, 0):
            copy.start()

    two = 2 * samples
    same = (
        lax.broadcasted_iota(jnp.int32, (two, two), 0) // samples
        == lax.broadcasted_iota(jnp.int32, (two, two), 1) // samples
    )

    def mix(query, other):
        raw = lax.dot_general(
            query, other, (((1,), (1,)), ((), ())), preferred_element_type=jnp.float32
        )
        raw = jnp.where(same, raw * scale, -1e30)
        raw = raw - jnp.max(raw, axis=-1, keepdims=True)
        weight = jnp.exp(raw)
        attend = (weight / jnp.sum(weight, axis=-1, keepdims=True)).astype(jnp.bfloat16)
        context = jnp.dot(attend, other, preferred_element_type=jnp.float32)
        return (query.astype(jnp.float32) + context).astype(jnp.bfloat16)

    def step_body(step, carry):
        slot = lax.rem(step, 2)

        @pl.when(step + 1 < steps)
        def _():
            for copy in copies(step + 1, 1 - slot):
                copy.start()

        for copy in copies(step, slot):
            copy.wait()
        for h in range(GROUP // 2):
            a = a_buf[slot, pl.ds(2 * h, 2)].reshape(two, features)
            b = b_buf[slot, pl.ds(2 * h, 2)].reshape(two, features)
            mixed[pl.ds(h * two, two)] = mix(a, b)
            mixed[pl.ds(GROUP * samples + h * two, two)] = mix(b, a)
        row = pl.multiple_of(step * 8, 8)
        for first in range(0, features, 256):
            hidden = jnp.tanh(
                jnp.dot(
                    mixed[...], w_mix[:, pl.ds(first, 256)], preferred_element_type=jnp.float32
                )
            )
            mean = jnp.sum(hidden.reshape(2 * GROUP, samples, 256), axis=1) * (1.0 / samples)
            pooled[pl.ds(row, 8), pl.ds(first, 256)] = mean
        return carry

    lax.fori_loop(0, steps, step_body, 0)

    def finish(chunk, carry):
        row = pl.multiple_of(chunk * 256, 256)
        vectors = pooled[pl.ds(row, 256)].astype(jnp.bfloat16)
        right = jnp.dot(vectors, w_pool[...], preferred_element_type=jnp.float32)
        left = pltpu.roll(right, 4, 0)
        inner = jnp.mean(left * right, axis=-1, keepdims=True)
        norms = (jnp.mean(left * left, axis=-1, keepdims=True) + EPSILON) * (
            jnp.mean(right * right, axis=-1, keepdims=True) + EPSILON
        )
        score = inner / jnp.sqrt(norms) / SOFTMAX_WARMTH
        hit = target[...] == row + lax.broadcasted_iota(jnp.int32, (256, 1024), 0)
        acc[...] += jnp.sum(jnp.where(hit, score, 0.0), axis=0, keepdims=True)
        return carry

    lax.fori_loop(0, (steps + 31) // 32, finish, 0)
    for k in range(8):
        out[k] = acc[:, pl.ds(128 * k, 128)]


def score_pairs(lst, target, w_mix, w_pool, sa, sb):
    samples, features = sa.shape[1:]
    vmem = pl.BlockSpec(memory_space=pltpu.VMEM)
    any_space = pl.BlockSpec(memory_space=pl.ANY)
    return pl.pallas_call(
        score_kernel,
        out_shape=jax.ShapeDtypeStruct((8, 1, 128), jnp.float32),
        in_specs=[
            pl.BlockSpec(memory_space=pltpu.SMEM), vmem, vmem, vmem, any_space, any_space,
        ],
        out_specs=vmem,
        scratch_shapes=[
            pltpu.VMEM((2, GROUP, samples, features), jnp.bfloat16),
            pltpu.VMEM((2, GROUP, samples, features), jnp.bfloat16),
            pltpu.VMEM((2 * GROUP * samples, features), jnp.bfloat16),
            pltpu.VMEM((2 * CAPACITY, features), jnp.float32),
            pltpu.VMEM((1, 1024), jnp.float32),
            pltpu.SemaphoreType.DMA((2, 2, GROUP)),
        ],
        name="score_pairs",
    )(lst, target, w_mix, w_pool, sa, sb)


def return_kernel(part, out, landed, send_sem, recv_sem):
    x, y, z, core = place()
    me = z * 8 + y * 2 + core

    def partner(k):
        return lax.rem(x + k // 4, 4), lax.rem(y + k % 4, 4)

    barrier = pltpu.get_barrier_semaphore()
    for k in range(1, 16):
        tx, ty = partner(k)
        pl.semaphore_signal(
            barrier, inc=1, device_id=(tx, z * 8 + ty * 2 + core), device_id_type=MESH
        )
    pl.semaphore_wait(barrier, 15)
    sent = []
    for k in range(1, 16):
        tx, ty = partner(k)
        copy = pltpu.make_async_remote_copy(
            src_ref=part.at[tx * 2 + ty // 2], dst_ref=landed.at[k],
            send_sem=send_sem.at[k], recv_sem=recv_sem.at[k],
            device_id=(tx, z * 8 + ty * 2 + core), device_id_type=MESH,
        )
        copy.start()
        sent.append(copy)
    total = part[x * 2 + y // 2]
    for k, copy in enumerate(sent, start=1):
        copy.wait_recv()
        total = total + landed[k]
    out[...] = total
    for copy in sent:
        copy.wait_send()


def return_scores(part):
    vmem = pl.BlockSpec(memory_space=pltpu.VMEM)
    return pl.pallas_call(
        return_kernel,
        out_shape=jax.ShapeDtypeStruct((1, 128), jnp.float32),
        in_specs=[vmem],
        out_specs=vmem,
        scratch_shapes=[
            pltpu.VMEM((16, 1, 128), jnp.float32),
            pltpu.SemaphoreType.DMA((16,)),
            pltpu.SemaphoreType.DMA((16,)),
        ],
        compiler_params=pltpu.CompilerParams(collective_id=1, has_side_effects=True),
        name="return_scores",
    )(part)


def my_pairs(plist):
    x, y, _, _ = place()
    codes = plist[:, :, 0, :64].reshape(1024)
    b = codes >> 6
    mine = (codes >= 0) & (((b >> 5) & 3) == y) & (((b >> 2) & 3) == x)
    entry = (codes & 63) + 64 * ((b >> 7) * 8 + ((b >> 4) & 1) * 4 + (b & 3))
    slot = jnp.arange(1024, dtype=jnp.int32)
    before = jnp.sum(jnp.where((slot[None, :] < slot[:, None]) & mine[None, :], 1, 0), axis=1)
    position = jnp.where(mine, before, -1)
    order = jnp.arange(CAPACITY, dtype=jnp.int32)
    entries = jnp.sum(jnp.where(position[None, :] == order[:, None], entry[None, :], 0), axis=1)
    count = jnp.sum(jnp.where(mine, 1, 0))
    target = jnp.where(mine, 8 * (before // GROUP) + 4 + before % GROUP, -1)
    lst = jnp.concatenate([entries, count[None], jnp.zeros((7,), jnp.int32)])
    return lst.astype(jnp.int32), target.reshape(1, 1024).astype(jnp.int32)


def local(cells, w_cell, w_mix, w_pool, pairs, counts):
    columns, samples, features = cells.shape
    pair_dev = pairs.shape[0]
    projected = jnp.dot(
        cells.reshape(columns * samples, features), w_cell, preferred_element_type=jnp.float32
    )
    projected = projected.astype(jnp.bfloat16).reshape(columns, samples, features)
    x, y, _, _ = place()
    slot = jnp.arange(pair_dev, dtype=jnp.int32)
    code = y * 16 + pairs[:, 0] % columns + 64 * pairs[:, 1]
    code = jnp.where(slot < counts[0], code, -1)
    code = jnp.concatenate([code, jnp.full((128 - pair_dev,), -1, jnp.int32)]).reshape(1, 128)
    sa, sb, plist = gather_blocks(projected, code)
    lst, target = my_pairs(plist)
    part = score_pairs(lst, target, w_mix, w_pool, sa, sb)
    whole = return_scores(part).reshape(128)
    return jnp.where(lax.rem(y, 2) == 0, whole[:64], whole[64:])


def solution(mesh):
    placed = (P("shard", None, None), P(), P(), P(), P(("grp", "shard"), None), P(("grp", "shard")))
    return jax.shard_map(
        local, mesh=mesh, in_specs=placed, out_specs=P(("grp", "shard")), check_vma=False
    )
```

time: 461 us -> 101 us (0.22)
  waiting for transfers between devices: 281 us -> 0 us
  matrix products: 103 us -> 3.86 us
  Pallas kernels: 0 us -> 88.3 us
  local copies, waits for them, and re-layouts: 29.8 us -> 0.78 us
  starting transfers between devices: 18.9 us -> 0 us
  other arithmetic: 22.9 us -> 6.72 us
    all_to_all x2 -> x0, waiting for transfers between devices: 281 us -> none  [the longest x1 274 us: local(): lax.all_to_all(found, 'shard', split_axis=0, concat_axis=0, tiled=True)]
    dot_general x49 -> x1, matrix products: 103 us -> 3.86 us  [local(): jnp.dot(cells.reshape(columns * samples, features), w_cell, preferred_ele...]
    pallas_call x0 -> x3, Pallas kernels: none -> 88.3 us  [the longest x1 44.4 us: gather_blocks(): pl.pallas_call(gather_kernel, out_shape=(jax.ShapeDtypeStruct((64, sample...]
    gather x10 -> x0, local copies, waits for them, and re-layouts: 28.2 us -> none  [the longest x8 11.8 us: score_block(): left_block = jnp.take(projected, left_sel, axis=0)]
    all_to_all x2 -> x0, starting transfers between devices: 18.9 us -> none  [the longest x1 13.1 us: local(): lax.all_to_all(requests, 'shard', split_axis=0, concat_axis=0, tiled=True)]
    select_n x7 -> x4, other arithmetic: 19 us -> 2.74 us  [the longest x1 1.34 us: local(): return jnp.where(lax.rem(y, 2) == 0, whole[:64], whole[64:])]
  transfers between devices with their start and end apart: 2 -> 0, of which waited for: 2 -> 0; matrix products, arithmetic and copies ran while one was open for 1% -> 0% of each run, Pallas kernels for 0% -> 0%
where the time goes in v1:
time: 101 us; the launch traced here: 100 us
  Pallas kernels  88.3 us (87%)
  other arithmetic  6.72 us (7%)
  matrix products  3.86 us (4%)
    pallas_call x1, Pallas kernels, gather_blocks(): pl.pallas_call(gather_kernel, out_shape=(jax.ShapeDtypeStruct((64, sample...  44.4 us
    pallas_call x1, Pallas kernels, score_pairs(): pl.pallas_call(score_kernel, out_shape=jax.ShapeDtypeStruct((8, 1, 128),...  35.8 us
    pallas_call x1, Pallas kernels, return_scores(): pl.pallas_call(return_kernel, out_shape=jax.ShapeDtypeStruct((1, 128), jn...  8.1 us
    dot_general x1, matrix products, local(): jnp.dot(cells.reshape(columns * samples, features), w_cell, preferred_ele...  3.86 us

profile of v1, /device:TPU:1, one launch (start us, length us, event | category | flops | bytes accessed | tf_op | source)
XLA Modules:
  0.0 100.5 jit_solution(1837451806536010874)
XLA Ops:
  0.0 0.0 copy-start
  0.8 0.8 compare_select_fusion.5
  1.5 0.5 pad_bitcast_fusion.code
  2.1 0.0 copy-done
  2.1 3.9 %convolution_convert_fusion = bf16[1024,768]{1,0:T(8,128)(2,1)} fusion(bf16[1024,768]{1,0:T(8,128)(2,1)S(1)} %bitcast.18, bf16[768,768]{1,0:T(8,128)(2,1)} %param.7), kind=kOutput, calls=%fused_computation.5 | convolution fusion | flops 1208745984 | bytes 4325376 | tf_op jit(solution)/shard_map/dot_general | solution.py:397
  5.9 44.4 %gather_blocks.1 = (bf16[64,64,768]{2,1,0:T(8,128)(2,1)}, bf16[64,64,768]{2,1,0:T(8,128)(2,1)}, s32[4,4,1,128]{3,2,1,0:T(1,128)}) custom-call(bf16[16,64,768]{2,1,0:T(8,128)(2,1)} %bitcast.19, s32[1,128]{1,0:T(1,128)} %pad_bitcast_fusion.code), custom_call_target="tpu_custom_call" | custom-call | tf_op jit(solution)/shard_map/gather_blocks/pallas_call | solution.py:192
  50.4 0.8 fusion.7
  51.1 0.1 reshape.222
  51.2 0.2 select_reduce_fusion
  51.4 0.1 reshape.224
  51.5 0.6 fusion.2.target
  52.2 0.8 add_reduce_fusion
  52.9 0.1 reshape.227
  53.0 0.3 select_reduce_fusion.1
  53.3 0.7 select_reduce_fusion.2
  53.9 1.3 %pad_add_fusion.lst = s32[520]{0:T(1024)} fusion(s32[7]{0:T(128)S(1)} %broadcast.329, s32[1]{0:T(128)} %bitcast.8, s32[512]{0:T(512)S(1)} %select_reduce_fusion.1), kind=kLoop, calls=%fused_computation.16 | loop fusion | flops 1040 | bytes 4160 | tf_op jit(solution)/shard_map/concatenate | solution.py:390
  55.2 35.8 %score_pairs.1.part = f32[8,1,128]{2,1,0:T(1,128)} custom-call(s32[520]{0:T(1024)} %pad_add_fusion.lst, s32[1,1024]{1,0:T(1,128)} %fusion.2.target, bf16[768,768]{1,0:T(8,128)(2,1)} %w_mix.1, bf16[768,768]{1,0:T(8,128)(2,1)} %w_pool.1, bf16[64,64,768]{2,1,0:T(8,128)(2,1)} %get-tuple-element.9.sa, bf16[64,64,768]{2,1,0:T(8,128)(2,1)} %get-tuple-element.10.sb), custom_call_target="tpu_custom_call" | custom-call | tf_op jit(solution)/shard_map/score_pairs/pallas_call | solution.py:308
  91.0 8.1 %return_scores.1 = f32[1,128]{1,0:T(1,128)} custom-call(f32[8,1,128]{2,1,0:T(1,128)} %score_pairs.1.part), custom_call_target="tpu_custom_call" | custom-call | tf_op jit(solution)/shard_map/return_scores/pallas_call | solution.py:362
  99.1 1.3 %fusion.3 = f32[64]{0:T(128)} fusion(pred[]{:T(512)S(6)} %eq.72, f32[1,128]{1,0:T(1,128)} %return_scores.1), kind=kLoop, calls=%fused_computation.23 | loop fusion | flops 64 | bytes 769 | tf_op jit(solution)/shard_map/jit(_where)/select_n | solution.py:410
  (3 shorter events, 0.0 us)
Async XLA Ops:
  0.0 2.1 %copy-start = (bf16[16,64,768]{2,1,0:T(8,128)(2,1)S(1)}, bf16[16,64,768]{2,1,0:T(8,128)(2,1)}, u32[]{:S(2)}) copy-start(bf16[16,64,768]{2,1,0:T(8,128)(2,1)} %param.6) | copy-start | bytes 4718596

commit v2 on v1

v2 whole, which is shorter than its diff:
```python
import functools
import math

import jax
import jax.numpy as jnp
from jax import lax
from jax.experimental import pallas as pl
from jax.experimental.pallas import tpu as pltpu
from jax.sharding import PartitionSpec as P

SOFTMAX_WARMTH = 0.07
EPSILON = 1e-06
MESH = pl.DeviceIdType.MESH
CAPACITY = 512
GROUP = 4


def place():
    x = lax.axis_index("grp")
    shard = lax.axis_index("shard")
    return x, lax.rem(shard // 2, 4), shard // 8, lax.rem(shard, 2)


def gather_kernel(
    cells, w_cell, w_mix, code, sa, sb, sa_mix, sb_mix, plist, stage, cell_w, mix_w,
    send_sem, recv_sem, local_sem
):
    columns, samples, features = stage.shape
    x, y, z, core = place()
    shard = lambda z_, y_, c_: z_ * 8 + y_ * 2 + c_
    xr, xl = lax.rem(x + 1, 4), lax.rem(x + 3, 4)
    yr, yl, yo = lax.rem(y + 1, 4), lax.rem(y + 3, 4), lax.rem(y + 2, 4)
    zs = [lax.rem(z + k, 8) for k in range(8)]
    me = shard(z, y, core)
    dev = {
        "x+": (xr, me),
        "x-": (xl, me),
        "y+": (x, shard(z, yr, core)),
        "y-": (x, shard(z, yl, core)),
        "z+": (x, shard(zs[1], y, core)),
        "z-": (x, shard(zs[7], y, core)),
        "c": (x, shard(z, y, 1 - core)),
    }
    barrier = pltpu.get_barrier_semaphore()
    for d in dev.values():
        pl.semaphore_signal(barrier, inc=1, device_id=d, device_id_type=MESH)

    loads = [
        pltpu.make_async_copy(cells, stage, local_sem.at[0]),
        pltpu.make_async_copy(w_cell, cell_w, local_sem.at[1]),
        pltpu.make_async_copy(w_mix, mix_w, local_sem.at[2]),
        pltpu.make_async_copy(code, plist.at[x, y], local_sem.at[3]),
    ]
    for copy in loads:
        copy.start()
    def project(quarter):
        rows = stage[pl.ds(quarter * 4, 4)].reshape(4 * samples, features)
        for first in range(0, features, 256):
            block = jnp.dot(
                rows, cell_w[:, pl.ds(first, 256)], preferred_element_type=jnp.float32
            ).astype(jnp.bfloat16)
            sa[pl.ds(y * 16 + quarter * 4, 4), :, pl.ds(first, 256)] = block.reshape(4, samples, 256)

    loads[0].wait()
    loads[1].wait()
    project(x)
    sb[pl.ds(z * 8 + core * 4, 4)] = sa[pl.ds(y * 16 + 4 * x, 4)]
    pl.semaphore_wait(barrier, len(dev))

    def times_mix(source, result, runs):
        rows = jnp.concatenate([source[pl.ds(*run)] for run in runs], axis=0)
        rows = rows.reshape(-1, features)
        for first in range(0, features, 256):
            block = jnp.dot(
                rows, mix_w[:, pl.ds(first, 256)], preferred_element_type=jnp.float32
            ).astype(jnp.bfloat16).reshape(-1, samples, 256)
            at = 0
            for start, size in runs:
                result[pl.ds(start, size), :, pl.ds(first, 256)] = block[at : at + size]
                at += size

    def mix_a(first_y, step_y, count, half):
        def body(k, carry):
            base = lax.rem(first_y + step_y * k, 4) * 16 + 2 * half
            times_mix(sa, sa_mix, [(base + 4 * q, 2) for q in range(4)])
            return carry
        lax.fori_loop(0, count, body, 0)

    def mix_b(d):
        def body(k, carry):
            times_mix(sb, sb_mix, [(lax.rem(z + 8 - d + 2 * d * k, 8) * 8, 8)])
            return carry
        lax.fori_loop(0, 1 if d in (0, 4) else 2, body, 0)

    kinds = {}
    sent = []

    def index_of(kind):
        return kinds.setdefault(kind, len(kinds))

    def send(kind, src, dst, to):
        k = index_of(kind)
        copy = pltpu.make_async_remote_copy(
            src_ref=src, dst_ref=dst, send_sem=send_sem.at[k], recv_sem=recv_sem.at[k],
            device_id=dev[to], device_id_type=MESH,
        )
        copy.start()
        sent.append(copy)

    def arrive(kind, slot, to):
        k = index_of(kind)
        pltpu.make_async_remote_copy(
            src_ref=slot, dst_ref=slot, send_sem=send_sem.at[k], recv_sem=recv_sem.at[k],
            device_id=dev[to], device_id_type=MESH,
        ).wait_recv()

    def a_cols(y_, first, size):
        return sa.at[pl.ds(y_ * 16 + first, size)]

    def b_cols(z_, c_, first, size):
        return sb.at[pl.ds(z_ * 8 + c_ * 4 + first, size)]

    def direct(y_, k):
        return a_cols(y_, 4 * lax.rem(x + k, 4) + 2, 2)

    def last(y_, k):
        return a_cols(y_, 4 * lax.rem(x + k, 4) + 3, 1)

    shared = a_cols(y, 4 * x, 2)
    loads[3].wait()
    send("l+", plist.at[x, y], plist.at[x, y], "y+")
    send("l-", plist.at[x, y], plist.at[x, y], "y-")
    for p in (0, 1):
        send(f"z+0{p}", b_cols(z, core, 2 * p, 2), b_cols(z, core, 2 * p, 2), "z+")
        send(f"z-0{p}", b_cols(z, core, 2 * (1 - p), 2), b_cols(z, core, 2 * (1 - p), 2), "z-")
        if p == 0:
            send("y+S", shared, shared, "y+")
            send("y-S", shared, shared, "y-")
    send("y+D0", direct(y, 0), direct(y, 0), "y+")
    send("y-D0", direct(y, 0), direct(y, 0), "y-")
    send("c0", b_cols(z, core, 0, 4), b_cols(z, core, 0, 4), "c")
    project(lax.rem(x + 1, 4))
    send("y+D1", direct(y, 1), direct(y, 1), "y+")
    send("y-D1", direct(y, 1), direct(y, 1), "y-")
    project(lax.rem(x + 2, 4))
    project(lax.rem(x + 3, 4))
    loads[2].wait()
    other = 1 - core
    arrive_c0 = lambda: arrive("c0", b_cols(z, other, 0, 4), "c")

    def arrive_c(d, p):
        arrive(f"c+{d}{p}", b_cols(zs[8 - d], other, 2 * p, 2), "c")
        arrive(f"c-{d}{p}", b_cols(zs[d], other, 2 * (1 - p), 2), "c")

    def z_round(d, p):
        up = b_cols(zs[8 - d], core, 2 * p, 2)
        down = b_cols(zs[d], core, 2 * (1 - p), 2)
        arrive(f"z+{d - 1}{p}", up, "z-")
        if d < 3 or (d == 3 and p == 0):
            send(f"z+{d}{p}", up, up, "z+")
        send(f"c+{d}{p}", up, up, "c")
        arrive(f"z-{d - 1}{p}", down, "z+")
        if d < 3 or (d == 3 and p == 0):
            send(f"z-{d}{p}", down, down, "z-")
        send(f"c-{d}{p}", down, down, "c")

    mix_a(y, 0, 1, 0)
    mix_a(y, 0, 1, 1)
    arrive_c0()
    mix_b(0)

    below, above = a_cols(yl, 4 * x, 2), a_cols(yr, 4 * x, 2)
    arrive("l+", plist.at[x, yl], "y-")
    send("l+2", plist.at[x, yl], plist.at[x, yl], "y+")
    arrive("l-", plist.at[x, yr], "y+")
    arrive("y+S", below, "y-")
    send("y+S2", below, below, "y+")
    send("x+b", below, below, "x+")
    send("x-b", below, below, "x-")
    arrive("y-S", above, "y+")
    send("x+a", above, above, "x+")
    send("x-a", above, above, "x-")
    z_round(1, 0)

    arrive("y+D0", direct(yl, 0), "y-")
    send("y+c", a_cols(yl, 4 * x + 2, 1), a_cols(yl, 4 * x + 2, 1), "y+")
    send("y+D2", direct(y, 2), direct(y, 2), "y+")
    send("y+D3", direct(y, 3), direct(y, 3), "y+")
    arrive("y-D0", direct(yr, 0), "y+")
    send("y-r0", last(yr, 0), last(yr, 0), "y-")
    send("y-D2", direct(y, 2), direct(y, 2), "y-")
    z_round(1, 1)
    arrive("l+2", plist.at[x, yo], "y-")
    send("lx+", plist.at[x], plist.at[x], "x+")
    send("lx-", plist.at[x], plist.at[x], "x-")

    got = a_cols(yl, 4 * xl, 2)
    arrive("x+b", got, "x-")
    send("x+b2", got, got, "x+")
    arrive_c(1, 0)
    arrive_c(1, 1)
    mix_b(1)
    z_round(2, 0)
    arrive("y-D1", direct(yr, 1), "y+")
    send("y-r1", last(yr, 1), last(yr, 1), "y-")
    send("y-D3", direct(y, 3), direct(y, 3), "y-")
    got = a_cols(yr, 4 * xr, 2)
    arrive("x-a", got, "x+")
    send("x-a2", got, got, "x-")
    arrive("lx+", plist.at[xl], "x-")
    send("lx+2", plist.at[xl], plist.at[xl], "x+")
    z_round(2, 1)

    arrive("y+S2", a_cols(yo, 4 * x, 2), "y-")
    for j in (0, 1):
        one, two = a_cols(yo, 4 * x + j, 1), a_cols(yo, 4 * x + 1 - j, 1)
        send(f"x+f{j}", one, one, "x+")
        send(f"x-f{1 - j}", two, two, "x-")
    arrive_c(2, 0)
    arrive_c(2, 1)
    mix_b(2)
    arrive("y+c", a_cols(yo, 4 * x + 2, 1), "y-")
    for to in ("x+", "x-"):
        send(to + "c", a_cols(yo, 4 * x + 2, 1), a_cols(yo, 4 * x + 2, 1), to)
    arrive("y-D2", direct(yr, 2), "y+")
    send("y-r2", last(yr, 2), last(yr, 2), "y-")
    z_round(3, 0)
    xo = lax.rem(x + 2, 4)
    arrive("x-b", a_cols(yl, 4 * xr, 2), "x+")
    arrive("x+a", a_cols(yr, 4 * xl, 2), "x-")
    arrive("x+b2", a_cols(yl, 4 * xo, 2), "x-")
    arrive("x-a2", a_cols(yr, 4 * xo, 2), "x+")
    got = a_cols(yo, 4 * xl, 1)
    arrive("x+f0", got, "x-")
    send("x+f02", got, got, "x+")
    got = a_cols(yo, 4 * xr + 1, 1)
    arrive("x-f1", got, "x+")
    send("x-f12", got, got, "x-")
    mix_a(yl, 2, 2, 0)
    z_round(3, 1)
    arrive("y-D3", direct(yr, 3), "y+")
    send("y-r3", last(yr, 3), last(yr, 3), "y-")
    got = a_cols(yo, 4 * xl + 2, 1)
    arrive("x+c", got, "x-")
    send("x+c2", got, got, "x+")
    mix_a(yr, 0, 1, 1)
    arrive_c(3, 0)
    arrive_c(3, 1)
    mix_b(3)
    for k in (1, 2, 3):
        arrive(f"y+D{k}", direct(yl, k), "y-")
    mix_a(yl, 0, 1, 1)

    z_round(4, 0)
    arrive("x+f1", a_cols(yo, 4 * xl + 1, 1), "x-")
    arrive("x-f0", a_cols(yo, 4 * xr, 1), "x+")
    arrive("x+f02", a_cols(yo, 4 * xo, 1), "x-")
    arrive("x-f12", a_cols(yo, 4 * xo + 1, 1), "x+")
    mix_a(yo, 0, 1, 0)
    arrive("x-c", a_cols(yo, 4 * xr + 2, 1), "x+")
    arrive("x+c2", a_cols(yo, 4 * xo + 2, 1), "x-")
    for k in range(4):
        arrive(f"y-r{k}", last(yo, k), "y+")
    mix_a(yo, 0, 1, 1)
    arrive_c(4, 0)
    mix_b(4)
    arrive("lx-", plist.at[xr], "x+")
    arrive("lx+2", plist.at[xo], "x-")
    for copy in sent:
        copy.wait_send()
    assert len(kinds) <= COPIES and len(kinds) == len(sent)


COPIES = 96


def gather_blocks(cells, w_cell, w_mix, code):
    vmem = pl.BlockSpec(memory_space=pltpu.VMEM)
    columns, samples, features = cells.shape
    blocks = pltpu.VMEM((64, samples, features), jnp.bfloat16)
    return pl.pallas_call(
        gather_kernel,
        out_shape=(blocks,) * 4 + (pltpu.VMEM((4, 4, 1, 128), jnp.int32),),
        in_specs=[pl.BlockSpec(memory_space=pltpu.HBM)] * 3 + [vmem],
        out_specs=(vmem,) * 5,
        scratch_shapes=[
            pltpu.VMEM((columns, samples, features), jnp.bfloat16),
            pltpu.VMEM(w_cell.shape, jnp.bfloat16),
            pltpu.VMEM(w_mix.shape, jnp.bfloat16),
            pltpu.SemaphoreType.DMA((COPIES,)),
            pltpu.SemaphoreType.DMA((COPIES,)),
            pltpu.SemaphoreType.DMA((4,)),
        ],
        compiler_params=pltpu.CompilerParams(
            collective_id=0, has_side_effects=True, vmem_limit_bytes=12 << 20
        ),
        name="gather_blocks",
    )(cells, w_cell, w_mix, code)


def score_kernel(
    sa, sb, sa_mix, sb_mix, plist, w_pool, out,
    pool_w, blend, pooled, target, table, lst, sem, list_sem
):
    samples, features = sa.shape[1:]
    scale = 1.0 / math.sqrt(features)
    load = pltpu.make_async_copy(w_pool, pool_w, sem)
    load.start()

    x, y, _, _ = place()
    codes = jnp.concatenate(
        [jnp.maximum(plist[k // 2, k % 2 * 2], plist[k // 2, k % 2 * 2 + 1]) for k in range(8)],
        axis=0,
    )
    b_id = codes >> 6
    mine = (codes >= 0) & (((b_id >> 5) & 3) == y) & (((b_id >> 2) & 3) == x)
    flag = jnp.where(mine, 1.0, 0.0)
    row_id = lax.broadcasted_iota(jnp.int32, (8, 128), 0)
    lane = lambda n: lax.broadcasted_iota(jnp.int32, (128, n), 1)
    upto = jnp.where(lax.broadcasted_iota(jnp.int32, (128, 128), 0) < lane(128), 1.0, 0.0)
    ahead = jnp.dot(
        flag.astype(jnp.bfloat16), upto.astype(jnp.bfloat16), preferred_element_type=jnp.float32
    )
    rows_upto = jnp.broadcast_to(jnp.sum(flag, axis=1, keepdims=True), (8, 128))
    own = rows_upto
    for shift in (1, 2, 4):
        rows_upto = rows_upto + jnp.where(
            row_id >= shift, pltpu.roll(rows_upto, shift, 0), 0.0
        )
    position = jnp.where(mine, (ahead + rows_upto - own).astype(jnp.int32), -1)
    target[...] = jnp.where(
        mine, 8 * (position >> 2) + 4 * ((position >> 1) & 1) + 2 + (position & 1), -1
    )
    spread = position.T
    a_at = (codes & 63).astype(jnp.bfloat16)
    b_at = ((b_id >> 7) * 8 + ((b_id >> 4) & 1) * 4 + (b_id & 3)).astype(jnp.bfloat16)
    found_a = jnp.zeros((8, CAPACITY), jnp.float32)
    found_b = jnp.zeros((8, CAPACITY), jnp.float32)
    for k in range(8):
        hit = jnp.where(spread[:, k : k + 1] == lane(CAPACITY), 1.0, 0.0).astype(jnp.bfloat16)
        keep = row_id == k
        both = jnp.concatenate(
            [jnp.where(keep, a_at, 0), jnp.where(keep, b_at, 0)], axis=0
        ).astype(jnp.bfloat16)
        got = jnp.dot(both, hit, preferred_element_type=jnp.float32)
        found_a = found_a + got[:8]
        found_b = found_b + got[8:]
    sum_rows = lambda v: jnp.sum(v, axis=0, keepdims=True).astype(jnp.int32)
    total = jnp.broadcast_to(rows_upto[7:, :1], (1, CAPACITY)).astype(jnp.int32)
    table[0] = sum_rows(found_a)
    table[1] = sum_rows(found_b)
    table[2] = total
    move = pltpu.make_async_copy(table, lst, list_sem)
    move.start()
    move.wait()
    count = lst[2, 0, 0]
    steps = (count + GROUP - 1) // GROUP

    two = 2 * samples
    same = (
        lax.broadcasted_iota(jnp.int32, (two, two), 0) // samples
        == lax.broadcasted_iota(jnp.int32, (two, two), 1) // samples
    )
    identity = jnp.where(
        lax.broadcasted_iota(jnp.int32, (two, two), 0) == lax.broadcasted_iota(jnp.int32, (two, two), 1),
        1.0, 0.0,
    ).astype(jnp.bfloat16)
    for h in range(GROUP // 2):
        blend[h, pl.ds(0, two), pl.ds(0, two)] = identity
        blend[h, pl.ds(two, two), pl.ds(two, two)] = identity

    def pair_rows(source, which, step, h):
        first = step * GROUP + 2 * h
        return jnp.concatenate(
            [source[lst[which, 0, first]], source[lst[which, 0, first + 1]]], axis=0
        )

    def scores(step, h):
        raw = lax.dot_general(
            pair_rows(sa, 0, step, h), pair_rows(sb, 1, step, h), (((1,), (1,)), ((), ())),
            preferred_element_type=jnp.float32,
        )
        return jnp.where(same, raw * scale, -1e30)

    def attend(raw, axis):
        weight = jnp.exp(raw - jnp.max(raw, axis=axis, keepdims=True))
        return weight * (1.0 / jnp.sum(weight, axis=axis, keepdims=True))

    def keep_weights(raw, h):
        blend[h, pl.ds(0, two), pl.ds(two, two)] = attend(raw, 1).astype(jnp.bfloat16)
        blend[h, pl.ds(two, two), pl.ds(0, two)] = attend(raw, 0).T.astype(jnp.bfloat16)

    def pool(step):
        products = [
            jnp.concatenate(
                [pair_rows(sa_mix, 0, step, h), pair_rows(sb_mix, 1, step, h)], axis=0
            )
            for h in range(GROUP // 2)
        ]
        row = pl.multiple_of(step * 2 * GROUP, 2 * GROUP)
        for first in range(0, features, 256):
            means = []
            for h in range(GROUP // 2):
                hidden = jnp.tanh(
                    jnp.dot(
                        blend[h], products[h][:, first : first + 256],
                        preferred_element_type=jnp.float32,
                    )
                )
                means.append(jnp.sum(hidden.reshape(4, samples, 256), axis=1) * (1.0 / samples))
            pooled[pl.ds(row, 2 * GROUP), pl.ds(first, 256)] = jnp.concatenate(means, axis=0)

    def step_body(step, carry):
        raw = [scores(step, h) for h in range(GROUP // 2)]
        pool(step - 1)
        for h in range(GROUP // 2):
            keep_weights(raw[h], h)
        return carry

    @pl.when(steps > 0)
    def _():
        raw = [scores(0, h) for h in range(GROUP // 2)]
        for h in range(GROUP // 2):
            keep_weights(raw[h], h)
        lax.fori_loop(1, steps, step_body, 0)
        pool(steps - 1)

    load.wait()
    out[...] = jnp.zeros_like(out)

    def finish(chunk, carry):
        row = pl.multiple_of(chunk * 256, 256)
        vectors = pooled[pl.ds(row, 256)].astype(jnp.bfloat16)
        right = jnp.dot(vectors, pool_w[...], preferred_element_type=jnp.float32)
        left = pltpu.roll(right, 2, 0)
        inner = jnp.mean(left * right, axis=-1, keepdims=True)
        norms = (jnp.mean(left * left, axis=-1, keepdims=True) + EPSILON) * (
            jnp.mean(right * right, axis=-1, keepdims=True) + EPSILON
        )
        score = inner / jnp.sqrt(norms) / SOFTMAX_WARMTH
        number = row + lax.broadcasted_iota(jnp.int32, (256, 128), 0)
        for k in range(8):
            hit = target[pl.ds(k, 1)] == number
            out[k] += jnp.sum(jnp.where(hit, score, 0.0), axis=0, keepdims=True)
        return carry

    lax.fori_loop(0, (steps + 31) // 32, finish, 0)


def score_pairs(sa, sb, sa_mix, sb_mix, plist, w_pool):
    samples, features = sa.shape[1:]
    vmem = pl.BlockSpec(memory_space=pltpu.VMEM)
    two = 2 * samples
    return pl.pallas_call(
        score_kernel,
        out_shape=pltpu.VMEM((8, 1, 128), jnp.float32),
        in_specs=[vmem] * 5 + [pl.BlockSpec(memory_space=pltpu.HBM)],
        out_specs=vmem,
        scratch_shapes=[
            pltpu.VMEM(w_pool.shape, jnp.bfloat16),
            pltpu.VMEM((GROUP // 2, 2 * two, 2 * two), jnp.bfloat16),
            pltpu.VMEM((2 * CAPACITY, features), jnp.float32),
            pltpu.VMEM((8, 128), jnp.int32),
            pltpu.VMEM((3, 1, CAPACITY), jnp.int32),
            pltpu.SMEM((3, 1, CAPACITY), jnp.int32),
            pltpu.SemaphoreType.DMA,
            pltpu.SemaphoreType.DMA,
        ],
        compiler_params=pltpu.CompilerParams(vmem_limit_bytes=16 << 20),
        name="score_pairs",
    )(sa, sb, sa_mix, sb_mix, plist, w_pool)


def return_kernel(part, out, landed, send_sem, recv_sem):
    x, y, z, core = place()
    me = z * 8 + y * 2 + core

    def partner(k):
        return lax.rem(x + k // 4, 4), lax.rem(y + k % 4, 4)

    barrier = pltpu.get_barrier_semaphore()
    for k in range(1, 16):
        tx, ty = partner(k)
        pl.semaphore_signal(
            barrier, inc=1, device_id=(tx, z * 8 + ty * 2 + core), device_id_type=MESH
        )
    pl.semaphore_wait(barrier, 15)
    sent = []
    for k in range(1, 16):
        tx, ty = partner(k)
        copy = pltpu.make_async_remote_copy(
            src_ref=part.at[tx * 2 + ty // 2], dst_ref=landed.at[k],
            send_sem=send_sem.at[k], recv_sem=recv_sem.at[k],
            device_id=(tx, z * 8 + ty * 2 + core), device_id_type=MESH,
        )
        copy.start()
        sent.append(copy)
    total = part[x * 2 + y // 2]
    for k, copy in enumerate(sent, start=1):
        copy.wait_recv()
        total = total + landed[k]
    half = jnp.where(lax.rem(y, 2) == 0, total, pltpu.roll(total, 64, 1))
    out[...] = half[:, :64]
    for copy in sent:
        copy.wait_send()


def return_scores(part):
    vmem = pl.BlockSpec(memory_space=pltpu.VMEM)
    return pl.pallas_call(
        return_kernel,
        out_shape=jax.ShapeDtypeStruct((1, 64), jnp.float32),
        in_specs=[vmem],
        out_specs=vmem,
        scratch_shapes=[
            pltpu.VMEM((16, 1, 128), jnp.float32),
            pltpu.SemaphoreType.DMA((16,)),
            pltpu.SemaphoreType.DMA((16,)),
        ],
        compiler_params=pltpu.CompilerParams(
            collective_id=1, has_side_effects=True, vmem_limit_bytes=1 << 20
        ),
        name="return_scores",
    )(part)


def local(cells, w_cell, w_mix, w_pool, pairs, counts):
    columns = cells.shape[0]
    pair_dev = pairs.shape[0]
    _, y, _, _ = place()
    slot = jnp.arange(pair_dev, dtype=jnp.int32)
    code = y * 16 + pairs[:, 0] % columns + 64 * pairs[:, 1]
    code = jnp.where(slot < counts[0], code, -1)
    odd = lax.rem(y, 2)
    code = jnp.concatenate([jnp.where(odd == 0, code, -1), jnp.where(odd == 1, code, -1)])
    cells, w_cell, w_mix, w_pool = [
        pltpu.with_memory_space_constraint(v, pltpu.HBM) for v in (cells, w_cell, w_mix, w_pool)
    ]
    blocks = gather_blocks(cells, w_cell, w_mix, code.reshape(1, 128))
    return return_scores(score_pairs(*blocks, w_pool)).reshape(pair_dev)


def solution(mesh):
    placed = (P("shard", None, None), P(), P(), P(), P(("grp", "shard"), None), P(("grp", "shard")))
    return jax.shard_map(
        local, mesh=mesh, in_specs=placed, out_specs=P(("grp", "shard")), check_vma=False
    )
```

time: 101 us -> 67.4 us (0.67)
  Pallas kernels: 88.3 us -> 65.8 us
  other arithmetic: 6.72 us -> 0.85 us
  matrix products: 3.86 us -> 0 us
    pallas_call x3, Pallas kernels: 88.3 us -> 65.8 us  [the longest x1 45.7 us: gather_blocks(): pl.pallas_call(gather_kernel, out_shape=(blocks,) * 4 + (pltpu.VMEM((4, 4...]
    dot_general x1 -> x0, matrix products: 3.86 us -> none  [local(): jnp.dot(cells.reshape(columns * samples, features), w_cell, preferred_ele...]
    select_n x4 -> x2, other arithmetic: 2.74 us -> 0.77 us  [the longest x1 0.77 us: local(): jnp.where(odd == 0, code, -1)]
    concatenate x1 -> x0, other arithmetic: 1.31 us -> none  [my_pairs(): lst = jnp.concatenate([entries, count[None], jnp.zeros((7,), jnp.int32)])]
    reduce_sum x3 -> x0, other arithmetic: 1.16 us -> none  [the longest x1 0.65 us: my_pairs(): count = jnp.sum(jnp.where(mine, 1, 0))]
where the time goes in v2:
time: 67.4 us; the launch traced here: 67.8 us
  Pallas kernels  65.8 us (98%)
  other arithmetic  0.85 us (1%)
  between operations  0.68 us (1%)
    pallas_call x1, Pallas kernels, gather_blocks(): pl.pallas_call(gather_kernel, out_shape=(blocks,) * 4 + (pltpu.VMEM((4, 4...  45.7 us
    pallas_call x1, Pallas kernels, score_pairs(): pl.pallas_call(score_kernel, out_shape=pltpu.VMEM((8, 1, 128), jnp.float3...  10.7 us
    pallas_call x1, Pallas kernels, return_scores(): pl.pallas_call(return_kernel, out_shape=jax.ShapeDtypeStruct((1, 64), jnp...  9.36 us

profile of v2, /device:TPU:1, one launch (start us, length us, event | category | flops | bytes accessed | tf_op | source)
XLA Modules:
  0.0 67.8 jit_solution(1129282280781619803)
XLA Ops:
  0.7 0.8 %broadcast_select_fusion.1 = (s32[64]{0:T(128)S(1)}, s32[64]{0:T(128)S(1)}) fusion(pred[]{:T(512)S(6)} %eq.8, s32[64,2]{0,1:T(2,128)} %param.10, s32[]{:T(128)S(6)} %mul.12, s32[]{:T(128)} %bitcast.10), kind=kLoop, calls=%fused_computation.5 | loop fusion | flops 1088 | bytes 1033 | tf_op jit(solution)/shard_map/jit(_where)/select_n | solution.py:535
  1.4 0.1 add_bitcast_fusion.code
  1.5 45.7 %gather_blocks.1 = (bf16[64,64,768]{2,1,0:T(8,128)(2,1)S(1)}, bf16[64,64,768]{2,1,0:T(8,128)(2,1)S(1)}, bf16[64,64,768]{2,1,0:T(8,128)(2,1)S(1)}, bf16[64,64,768]{2,1,0:T(8,128)(2,1)S(1)}, s32[4,4,1,128]{3,2,1,0:T(1,128)S(1)}) custom-call(bf16[16,64,768]{2,1,0:T(8,128)(2,1)} %cells.1, bf16[768,768]{1,0:T(8,128)(2,1)} %w_cell.1, bf16[768,768]{1,0:T(8,128)(2,1)} %w_mix.1, ...), custom_call_target="tpu_custom_call" | custom-call | tf_op jit(solution)/shard_map/gather_blocks/pallas_call | solution.py:281
  47.3 10.7 %score_pairs.1.part = f32[8,1,128]{2,1,0:T(1,128)S(1)} custom-call(bf16[64,64,768]{2,1,0:T(8,128)(2,1)S(1)} %get-tuple-element.10.sa, bf16[64,64,768]{2,1,0:T(8,128)(2,1)S(1)} %get-tuple-element.11.sb, bf16[64,64,768]{2,1,0:T(8,128)(2,1)S(1)} %get-tuple-element.12.sa_mix, bf16[64,64,768]{2,1,0:T(8,128)(2,1)S(1)} %get-tuple-element.13.sb_mix, ...), custom_call_target="tpu_custom_call" | custom-call | tf_op jit(solution)/shard_map/score_pairs/pallas_call | solution.py:454
  57.9 9.4 %return_scores.1 = f32[1,64]{1,0:T(1,128)S(1)} custom-call(f32[8,1,128]{2,1,0:T(1,128)S(1)} %score_pairs.1.part), custom_call_target="tpu_custom_call" | custom-call | tf_op jit(solution)/shard_map/return_scores/pallas_call | solution.py:510
  67.3 0.5 copy.9
  (1 shorter events, 0.0 us)

commit v3 on v2

--- a/solution.py
+++ b/solution.py
@@ -22,8 +22,8 @@
 
 
 def gather_kernel(
-    cells, w_cell, w_mix, code, sa, sb, sa_mix, sb_mix, plist, stage, cell_w, mix_w,
-    send_sem, recv_sem, local_sem
+    cells, w_cell, w_mix, pairs, live, sa, sb, sa_mix, sb_mix, plist, stage, cell_w, mix_w,
+    ids, send_sem, recv_sem, local_sem
 ):
     columns, samples, features = stage.shape
     x, y, z, core = place()
@@ -45,25 +45,38 @@
     for d in dev.values():
         pl.semaphore_signal(barrier, inc=1, device_id=d, device_id_type=MESH)
 
+    quarter_at = lambda k: pl.ds(4 * lax.rem(x + k, 4), 4)
+    thirds = range(0, features, 256)
+    moves = [(pairs, ids), (cells.at[quarter_at(0)], stage.at[quarter_at(0)])]
+    moves += [(w_cell.at[:, pl.ds(f, 256)], cell_w.at[:, pl.ds(f, 256)]) for f in thirds]
+    moves += [(cells.at[quarter_at(k)], stage.at[quarter_at(k)]) for k in (1, 2, 3)]
+    moves += [(w_mix, mix_w)]
     loads = [
-        pltpu.make_async_copy(cells, stage, local_sem.at[0]),
-        pltpu.make_async_copy(w_cell, cell_w, local_sem.at[1]),
-        pltpu.make_async_copy(w_mix, mix_w, local_sem.at[2]),
-        pltpu.make_async_copy(code, plist.at[x, y], local_sem.at[3]),
+        pltpu.make_async_copy(src, dst, local_sem.at[k]) for k, (src, dst) in enumerate(moves)
     ]
     for copy in loads:
         copy.start()
-    def project(quarter):
+
+    loads[0].wait()
+    first_id, second_id = ids[pl.ds(0, 1)], ids[pl.ds(1, 1)]
+    slot = lax.broadcasted_iota(jnp.int32, first_id.shape, 1)
+    row = jnp.where(slot < live[0], y * 16 + (first_id & 15) + 64 * second_id, -1)
+    row = jnp.concatenate([row, jnp.full(row.shape, -1, jnp.int32)], axis=1)
+    plist[x, y] = jnp.where(lax.rem(y, 2) == 0, row, pltpu.roll(row, 64, 1))
+
+    def project(k):
+        quarter = lax.rem(x + k, 4)
+        loads[1 if k == 0 else 4 + k].wait()
         rows = stage[pl.ds(quarter * 4, 4)].reshape(4 * samples, features)
-        for first in range(0, features, 256):
+        for third, first in enumerate(thirds):
+            if k == 0:
+                loads[2 + third].wait()
             block = jnp.dot(
                 rows, cell_w[:, pl.ds(first, 256)], preferred_element_type=jnp.float32
             ).astype(jnp.bfloat16)
             sa[pl.ds(y * 16 + quarter * 4, 4), :, pl.ds(first, 256)] = block.reshape(4, samples, 256)
 
-    loads[0].wait()
-    loads[1].wait()
-    project(x)
+    project(0)
     sb[pl.ds(z * 8 + core * 4, 4)] = sa[pl.ds(y * 16 + 4 * x, 4)]
     pl.semaphore_wait(barrier, len(dev))
 
@@ -90,7 +103,10 @@
         def body(k, carry):
             times_mix(sb, sb_mix, [(lax.rem(z + 8 - d + 2 * d * k, 8) * 8, 8)])
             return carry
-        lax.fori_loop(0, 1 if d in (0, 4) else 2, body, 0)
+        lax.fori_loop(0, 1 if d == 0 else 2, body, 0)
+
+    def mix_far(c_):
+        times_mix(sb, sb_mix, [(zs[4] * 8 + c_ * 4, 4)])
 
     kinds = {}
     sent = []
@@ -127,7 +143,6 @@
         return a_cols(y_, 4 * lax.rem(x + k, 4) + 3, 1)
 
     shared = a_cols(y, 4 * x, 2)
-    loads[3].wait()
     send("l+", plist.at[x, y], plist.at[x, y], "y+")
     send("l-", plist.at[x, y], plist.at[x, y], "y-")
     for p in (0, 1):
@@ -139,12 +154,11 @@
     send("y+D0", direct(y, 0), direct(y, 0), "y+")
     send("y-D0", direct(y, 0), direct(y, 0), "y-")
     send("c0", b_cols(z, core, 0, 4), b_cols(z, core, 0, 4), "c")
-    project(lax.rem(x + 1, 4))
-    send("y+D1", direct(y, 1), direct(y, 1), "y+")
+    project(1)
     send("y-D1", direct(y, 1), direct(y, 1), "y-")
-    project(lax.rem(x + 2, 4))
-    project(lax.rem(x + 3, 4))
-    loads[2].wait()
+    project(2)
+    project(3)
+    loads[8].wait()
     other = 1 - core
     arrive_c0 = lambda: arrive("c0", b_cols(z, other, 0, 4), "c")
 
@@ -184,8 +198,8 @@
 
     arrive("y+D0", direct(yl, 0), "y-")
     send("y+c", a_cols(yl, 4 * x + 2, 1), a_cols(yl, 4 * x + 2, 1), "y+")
-    send("y+D2", direct(y, 2), direct(y, 2), "y+")
-    send("y+D3", direct(y, 3), direct(y, 3), "y+")
+    for k in (1, 2, 3):
+        send(f"y+D{k}", direct(y, k), direct(y, k), "y+")
     arrive("y-D0", direct(yr, 0), "y+")
     send("y-r0", last(yr, 0), last(yr, 0), "y-")
     send("y-D2", direct(y, 2), direct(y, 2), "y-")
@@ -193,14 +207,19 @@
     arrive("l+2", plist.at[x, yo], "y-")
     send("lx+", plist.at[x], plist.at[x], "x+")
     send("lx-", plist.at[x], plist.at[x], "x-")
-
+    arrive_c(1, 0)
+    arrive_c(1, 1)
+    mix_b(1)
+
+    arrive("y+S2", a_cols(yo, 4 * x, 2), "y-")
+    for j in (0, 1):
+        one, two = a_cols(yo, 4 * x + j, 1), a_cols(yo, 4 * x + 1 - j, 1)
+        send(f"x+f{j}", one, one, "x+")
+        send(f"x-f{1 - j}", two, two, "x-")
+    z_round(2, 0)
     got = a_cols(yl, 4 * xl, 2)
     arrive("x+b", got, "x-")
     send("x+b2", got, got, "x+")
-    arrive_c(1, 0)
-    arrive_c(1, 1)
-    mix_b(1)
-    z_round(2, 0)
     arrive("y-D1", direct(yr, 1), "y+")
     send("y-r1", last(yr, 1), last(yr, 1), "y-")
     send("y-D3", direct(y, 3), direct(y, 3), "y-")
@@ -209,40 +228,36 @@
     send("x-a2", got, got, "x-")
     arrive("lx+", plist.at[xl], "x-")
     send("lx+2", plist.at[xl], plist.at[xl], "x+")
+    arrive("y+c", a_cols(yo, 4 * x + 2, 1), "y-")
+    for to in ("x+", "x-"):
+        send(to + "c", a_cols(yo, 4 * x + 2, 1), a_cols(yo, 4 * x + 2, 1), to)
     z_round(2, 1)
 
-    arrive("y+S2", a_cols(yo, 4 * x, 2), "y-")
-    for j in (0, 1):
-        one, two = a_cols(yo, 4 * x + j, 1), a_cols(yo, 4 * x + 1 - j, 1)
-        send(f"x+f{j}", one, one, "x+")
-        send(f"x-f{1 - j}", two, two, "x-")
     arrive_c(2, 0)
     arrive_c(2, 1)
     mix_b(2)
-    arrive("y+c", a_cols(yo, 4 * x + 2, 1), "y-")
-    for to in ("x+", "x-"):
-        send(to + "c", a_cols(yo, 4 * x + 2, 1), a_cols(yo, 4 * x + 2, 1), to)
+    early = len(sent)
     arrive("y-D2", direct(yr, 2), "y+")
     send("y-r2", last(yr, 2), last(yr, 2), "y-")
+    got = a_cols(yo, 4 * xl, 1)
+    arrive("x+f0", got, "x-")
+    send("x+f02", got, got, "x+")
+    got = a_cols(yo, 4 * xr + 1, 1)
+    arrive("x-f1", got, "x+")
+    send("x-f12", got, got, "x-")
     z_round(3, 0)
     xo = lax.rem(x + 2, 4)
     arrive("x-b", a_cols(yl, 4 * xr, 2), "x+")
     arrive("x+a", a_cols(yr, 4 * xl, 2), "x-")
     arrive("x+b2", a_cols(yl, 4 * xo, 2), "x-")
     arrive("x-a2", a_cols(yr, 4 * xo, 2), "x+")
-    got = a_cols(yo, 4 * xl, 1)
-    arrive("x+f0", got, "x-")
-    send("x+f02", got, got, "x+")
-    got = a_cols(yo, 4 * xr + 1, 1)
-    arrive("x-f1", got, "x+")
-    send("x-f12", got, got, "x-")
     mix_a(yl, 2, 2, 0)
+    got = a_cols(yo, 4 * xl + 2, 1)
+    arrive("x+c", got, "x-")
+    send("x+c2", got, got, "x+")
     z_round(3, 1)
     arrive("y-D3", direct(yr, 3), "y+")
     send("y-r3", last(yr, 3), last(yr, 3), "y-")
-    got = a_cols(yo, 4 * xl + 2, 1)
-    arrive("x+c", got, "x-")
-    send("x+c2", got, got, "x+")
     mix_a(yr, 0, 1, 1)
     arrive_c(3, 0)
     arrive_c(3, 1)
@@ -250,57 +265,64 @@
     for k in (1, 2, 3):
         arrive(f"y+D{k}", direct(yl, k), "y-")
     mix_a(yl, 0, 1, 1)
-
-    z_round(4, 0)
     arrive("x+f1", a_cols(yo, 4 * xl + 1, 1), "x-")
     arrive("x-f0", a_cols(yo, 4 * xr, 1), "x+")
     arrive("x+f02", a_cols(yo, 4 * xo, 1), "x-")
     arrive("x-f12", a_cols(yo, 4 * xo + 1, 1), "x+")
     mix_a(yo, 0, 1, 0)
+    arrive("lx-", plist.at[xr], "x+")
+    arrive("lx+2", plist.at[xo], "x-")
+    for copy in sent[:early]:
+        copy.wait_send()
+
+    z_round(4, 0)
     arrive("x-c", a_cols(yo, 4 * xr + 2, 1), "x+")
     arrive("x+c2", a_cols(yo, 4 * xo + 2, 1), "x-")
     for k in range(4):
         arrive(f"y-r{k}", last(yo, k), "y+")
     mix_a(yo, 0, 1, 1)
+    mix_far(core)
+    for copy in sent[early:-2]:
+        copy.wait_send()
     arrive_c(4, 0)
-    mix_b(4)
-    arrive("lx-", plist.at[xr], "x+")
-    arrive("lx+2", plist.at[xo], "x-")
+    mix_far(other)
+    sent[:-2] = []
     for copy in sent:
         copy.wait_send()
-    assert len(kinds) <= COPIES and len(kinds) == len(sent)
+    assert len(kinds) <= COPIES
 
 
 COPIES = 96
 
 
-def gather_blocks(cells, w_cell, w_mix, code):
+def gather_blocks(cells, w_cell, w_mix, pairs, counts):
     vmem = pl.BlockSpec(memory_space=pltpu.VMEM)
     columns, samples, features = cells.shape
     blocks = pltpu.VMEM((64, samples, features), jnp.bfloat16)
     return pl.pallas_call(
         gather_kernel,
         out_shape=(blocks,) * 4 + (pltpu.VMEM((4, 4, 1, 128), jnp.int32),),
-        in_specs=[pl.BlockSpec(memory_space=pltpu.HBM)] * 3 + [vmem],
+        in_specs=[pl.BlockSpec(memory_space=pltpu.HBM)] * 4 + [pl.BlockSpec(memory_space=pltpu.SMEM)],
         out_specs=(vmem,) * 5,
         scratch_shapes=[
             pltpu.VMEM((columns, samples, features), jnp.bfloat16),
             pltpu.VMEM(w_cell.shape, jnp.bfloat16),
             pltpu.VMEM(w_mix.shape, jnp.bfloat16),
+            pltpu.VMEM(pairs.shape, jnp.int32),
             pltpu.SemaphoreType.DMA((COPIES,)),
             pltpu.SemaphoreType.DMA((COPIES,)),
-            pltpu.SemaphoreType.DMA((4,)),
+            pltpu.SemaphoreType.DMA((9,)),
         ],
         compiler_params=pltpu.CompilerParams(
             collective_id=0, has_side_effects=True, vmem_limit_bytes=12 << 20
         ),
         name="gather_blocks",
-    )(cells, w_cell, w_mix, code)
+    )(cells, w_cell, w_mix, pairs, counts)
 
 
 def score_kernel(
     sa, sb, sa_mix, sb_mix, plist, w_pool, out,
-    pool_w, blend, pooled, target, table, lst, sem, list_sem
+    pool_w, raw, blend, pooled, target, table, lst, sem, list_sem
 ):
     samples, features = sa.shape[1:]
     scale = 1.0 / math.sqrt(features)
@@ -376,19 +398,19 @@
         )
 
     def scores(step, h):
-        raw = lax.dot_general(
+        found = lax.dot_general(
             pair_rows(sa, 0, step, h), pair_rows(sb, 1, step, h), (((1,), (1,)), ((), ())),
             preferred_element_type=jnp.float32,
         )
-        return jnp.where(same, raw * scale, -1e30)
-
-    def attend(raw, axis):
-        weight = jnp.exp(raw - jnp.max(raw, axis=axis, keepdims=True))
+        return jnp.where(same, found * scale, -1e30)
+
+    def attend(found, axis):
+        weight = jnp.exp(found - jnp.max(found, axis=axis, keepdims=True))
         return weight * (1.0 / jnp.sum(weight, axis=axis, keepdims=True))
 
-    def keep_weights(raw, h):
-        blend[h, pl.ds(0, two), pl.ds(two, two)] = attend(raw, 1).astype(jnp.bfloat16)
-        blend[h, pl.ds(two, two), pl.ds(0, two)] = attend(raw, 0).T.astype(jnp.bfloat16)
+    def keep_weights(found, h):
+        blend[h, pl.ds(0, two), pl.ds(two, two)] = attend(found, 1).astype(jnp.bfloat16)
+        blend[h, pl.ds(two, two), pl.ds(0, two)] = attend(found, 0).T.astype(jnp.bfloat16)
 
     def pool(step):
         products = [
@@ -410,18 +432,26 @@
                 means.append(jnp.sum(hidden.reshape(4, samples, 256), axis=1) * (1.0 / samples))
             pooled[pl.ds(row, 2 * GROUP), pl.ds(first, 256)] = jnp.concatenate(means, axis=0)
 
+    halves = range(GROUP // 2)
+
+    def keep_scores(step):
+        for h in halves:
+            raw[h] = scores(step, h)
+
     def step_body(step, carry):
-        raw = [scores(step, h) for h in range(GROUP // 2)]
+        now = [raw[h] for h in halves]
         pool(step - 1)
-        for h in range(GROUP // 2):
-            keep_weights(raw[h], h)
+        for h in halves:
+            keep_weights(now[h], h)
+        keep_scores(jnp.minimum(step + 1, steps - 1))
         return carry
 
     @pl.when(steps > 0)
     def _():
-        raw = [scores(0, h) for h in range(GROUP // 2)]
-        for h in range(GROUP // 2):
+        keep_scores(0)
+        for h in halves:
             keep_weights(raw[h], h)
+        keep_scores(jnp.minimum(1, steps - 1))
         lax.fori_loop(1, steps, step_body, 0)
         pool(steps - 1)
 
@@ -434,9 +464,8 @@
         right = jnp.dot(vectors, pool_w[...], preferred_element_type=jnp.float32)
         left = pltpu.roll(right, 2, 0)
         inner = jnp.mean(left * right, axis=-1, keepdims=True)
-        norms = (jnp.mean(left * left, axis=-1, keepdims=True) + EPSILON) * (
-            jnp.mean(right * right, axis=-1, keepdims=True) + EPSILON
-        )
+        size = jnp.mean(right * right, axis=-1, keepdims=True) + EPSILON
+        norms = size * pltpu.roll(size, 2, 0)
         score = inner / jnp.sqrt(norms) / SOFTMAX_WARMTH
         number = row + lax.broadcasted_iota(jnp.int32, (256, 128), 0)
         for k in range(8):
@@ -458,6 +487,7 @@
         out_specs=vmem,
         scratch_shapes=[
             pltpu.VMEM(w_pool.shape, jnp.bfloat16),
+            pltpu.VMEM((GROUP // 2, two, two), jnp.float32),
             pltpu.VMEM((GROUP // 2, 2 * two, 2 * two), jnp.bfloat16),
             pltpu.VMEM((2 * CAPACITY, features), jnp.float32),
             pltpu.VMEM((8, 128), jnp.int32),
@@ -525,19 +555,10 @@
 
 
 def local(cells, w_cell, w_mix, w_pool, pairs, counts):
-    columns = cells.shape[0]
-    pair_dev = pairs.shape[0]
-    _, y, _, _ = place()
-    slot = jnp.arange(pair_dev, dtype=jnp.int32)
-    code = y * 16 + pairs[:, 0] % columns + 64 * pairs[:, 1]
-    code = jnp.where(slot < counts[0], code, -1)
-    odd = lax.rem(y, 2)
-    code = jnp.concatenate([jnp.where(odd == 0, code, -1), jnp.where(odd == 1, code, -1)])
-    cells, w_cell, w_mix, w_pool = [
-        pltpu.with_memory_space_constraint(v, pltpu.HBM) for v in (cells, w_cell, w_mix, w_pool)
-    ]
-    blocks = gather_blocks(cells, w_cell, w_mix, code.reshape(1, 128))
-    return return_scores(score_pairs(*blocks, w_pool)).reshape(pair_dev)
+    in_place = lambda v: pltpu.with_memory_space_constraint(v, pltpu.HBM)
+    cells, w_cell, w_mix, w_pool = map(in_place, (cells, w_cell, w_mix, w_pool))
+    blocks = gather_blocks(cells, w_cell, w_mix, in_place(pairs.T), counts)
+    return return_scores(score_pairs(*blocks, w_pool)).reshape(pairs.shape[0])
 
 
 def solution(mesh):

time: 67.4 us -> 65.4 us (0.970)
  Pallas kernels: 65.8 us -> 64.5 us
  other arithmetic: 0.85 us -> 0 us
    pallas_call x1, Pallas kernels: 9.36 us -> 7 us  [return_scores(): pl.pallas_call(return_kernel, out_shape=jax.ShapeDtypeStruct((1, 64), jnp...]
    pallas_call x1, Pallas kernels: 45.7 us -> 48.1 us  [gather_blocks(): pl.pallas_call(gather_kernel, out_shape=(blocks,) * 4 + (pltpu.VMEM((4, 4...]
    pallas_call x1, Pallas kernels: 10.7 us -> 9.38 us  [score_pairs(): pl.pallas_call(score_kernel, out_shape=pltpu.VMEM((8, 1, 128), jnp.float3...]
    select_n x2 -> x0, other arithmetic: 0.77 us -> none  [the longest x1 0.77 us: local(): jnp.where(odd == 0, code, -1)]
where the time goes in v3:
time: 65.4 us; the launch traced here: 65.6 us
  Pallas kernels  64.5 us (99%)
  between operations  0.68 us (1%)
    pallas_call x1, Pallas kernels, gather_blocks(): pl.pallas_call(gather_kernel, out_shape=(blocks,) * 4 + (pltpu.VMEM((4, 4...  48.1 us
    pallas_call x1, Pallas kernels, score_pairs(): pl.pallas_call(score_kernel, out_shape=pltpu.VMEM((8, 1, 128), jnp.float3...  9.38 us
    pallas_call x1, Pallas kernels, return_scores(): pl.pallas_call(return_kernel, out_shape=jax.ShapeDtypeStruct((1, 64), jnp...  7 us

profile of v3, /device:TPU:1, one launch (start us, length us, event | category | flops | bytes accessed | tf_op | source)
XLA Modules:
  0.0 65.6 jit_solution(14696518339576248213)
XLA Ops:
  0.7 48.1 %gather_blocks.1 = (bf16[64,64,768]{2,1,0:T(8,128)(2,1)S(1)}, bf16[64,64,768]{2,1,0:T(8,128)(2,1)S(1)}, bf16[64,64,768]{2,1,0:T(8,128)(2,1)S(1)}, bf16[64,64,768]{2,1,0:T(8,128)(2,1)S(1)}, s32[4,4,1,128]{3,2,1,0:T(1,128)S(1)}) custom-call(bf16[16,64,768]{2,1,0:T(8,128)(2,1)} %cells.1, bf16[768,768]{1,0:T(8,128)(2,1)} %w_cell.1, bf16[768,768]{1,0:T(8,128)(2,1)} %w_mix.1, ...), custom_call_target="tpu_custom_call" | custom-call | tf_op jit(solution)/shard_map/gather_blocks/pallas_call | solution.py:302
  48.7 9.4 %score_pairs.1.part = f32[8,1,128]{2,1,0:T(1,128)S(1)} custom-call(bf16[64,64,768]{2,1,0:T(8,128)(2,1)S(1)} %get-tuple-element.10.sa, bf16[64,64,768]{2,1,0:T(8,128)(2,1)S(1)} %get-tuple-element.11.sb, bf16[64,64,768]{2,1,0:T(8,128)(2,1)S(1)} %get-tuple-element.12.sa_mix, bf16[64,64,768]{2,1,0:T(8,128)(2,1)S(1)} %get-tuple-element.13.sb_mix, ...), custom_call_target="tpu_custom_call" | custom-call | tf_op jit(solution)/shard_map/score_pairs/pallas_call | solution.py:483
  58.1 7.0 %return_scores.1 = f32[1,64]{1,0:T(1,128)S(1)} custom-call(f32[8,1,128]{2,1,0:T(1,128)S(1)} %score_pairs.1.part), custom_call_target="tpu_custom_call" | custom-call | tf_op jit(solution)/shard_map/return_scores/pallas_call | solution.py:540
  65.1 0.5 copy.9

commit v4 on v3

--- a/solution.py
+++ b/solution.py
@@ -27,6 +27,18 @@
 ):
     columns, samples, features = stage.shape
     x, y, z, core = place()
+    quarter_at = lambda k: pl.ds(4 * lax.rem(x + k, 4), 4)
+    thirds = range(0, features, 256)
+    moves = [(pairs, ids), (cells.at[quarter_at(0)], stage.at[quarter_at(0)])]
+    moves += [(w_cell.at[:, pl.ds(f, 256)], cell_w.at[:, pl.ds(f, 256)]) for f in thirds]
+    moves += [(cells.at[quarter_at(k)], stage.at[quarter_at(k)]) for k in (1, 2, 3)]
+    moves += [(w_mix, mix_w)]
+    loads = [
+        pltpu.make_async_copy(src, dst, local_sem.at[k]) for k, (src, dst) in enumerate(moves)
+    ]
+    for copy in loads:
+        copy.start()
+
     shard = lambda z_, y_, c_: z_ * 8 + y_ * 2 + c_
     xr, xl = lax.rem(x + 1, 4), lax.rem(x + 3, 4)
     yr, yl, yo = lax.rem(y + 1, 4), lax.rem(y + 3, 4), lax.rem(y + 2, 4)
@@ -45,25 +57,6 @@
     for d in dev.values():
         pl.semaphore_signal(barrier, inc=1, device_id=d, device_id_type=MESH)
 
-    quarter_at = lambda k: pl.ds(4 * lax.rem(x + k, 4), 4)
-    thirds = range(0, features, 256)
-    moves = [(pairs, ids), (cells.at[quarter_at(0)], stage.at[quarter_at(0)])]
-    moves += [(w_cell.at[:, pl.ds(f, 256)], cell_w.at[:, pl.ds(f, 256)]) for f in thirds]
-    moves += [(cells.at[quarter_at(k)], stage.at[quarter_at(k)]) for k in (1, 2, 3)]
-    moves += [(w_mix, mix_w)]
-    loads = [
-        pltpu.make_async_copy(src, dst, local_sem.at[k]) for k, (src, dst) in enumerate(moves)
-    ]
-    for copy in loads:
-        copy.start()
-
-    loads[0].wait()
-    first_id, second_id = ids[pl.ds(0, 1)], ids[pl.ds(1, 1)]
-    slot = lax.broadcasted_iota(jnp.int32, first_id.shape, 1)
-    row = jnp.where(slot < live[0], y * 16 + (first_id & 15) + 64 * second_id, -1)
-    row = jnp.concatenate([row, jnp.full(row.shape, -1, jnp.int32)], axis=1)
-    plist[x, y] = jnp.where(lax.rem(y, 2) == 0, row, pltpu.roll(row, 64, 1))
-
     def project(k):
         quarter = lax.rem(x + k, 4)
         loads[1 if k == 0 else 4 + k].wait()
@@ -78,35 +71,14 @@
 
     project(0)
     sb[pl.ds(z * 8 + core * 4, 4)] = sa[pl.ds(y * 16 + 4 * x, 4)]
+    loads[0].wait()
+    first_id, second_id = ids[pl.ds(0, 1)], ids[pl.ds(1, 1)]
+    slot = lax.broadcasted_iota(jnp.int32, first_id.shape, 1)
+    row = jnp.where(slot < live[0], y * 16 + (first_id & 15) + 64 * second_id, -1)
+    row = jnp.concatenate([row, jnp.full(row.shape, -1, jnp.int32)], axis=1)
+    plist[x, y] = jnp.where(lax.rem(y, 2) == 0, row, pltpu.roll(row, 64, 1))
+
     pl.semaphore_wait(barrier, len(dev))
-
-    def times_mix(source, result, runs):
-        rows = jnp.concatenate([source[pl.ds(*run)] for run in runs], axis=0)
-        rows = rows.reshape(-1, features)
-        for first in range(0, features, 256):
-            block = jnp.dot(
-                rows, mix_w[:, pl.ds(first, 256)], preferred_element_type=jnp.float32
-            ).astype(jnp.bfloat16).reshape(-1, samples, 256)
-            at = 0
-            for start, size in runs:
-                result[pl.ds(start, size), :, pl.ds(first, 256)] = block[at : at + size]
-                at += size
-
-    def mix_a(first_y, step_y, count, half):
-        def body(k, carry):
-            base = lax.rem(first_y + step_y * k, 4) * 16 + 2 * half
-            times_mix(sa, sa_mix, [(base + 4 * q, 2) for q in range(4)])
-            return carry
-        lax.fori_loop(0, count, body, 0)
-
-    def mix_b(d):
-        def body(k, carry):
-            times_mix(sb, sb_mix, [(lax.rem(z + 8 - d + 2 * d * k, 8) * 8, 8)])
-            return carry
-        lax.fori_loop(0, 1 if d == 0 else 2, body, 0)
-
-    def mix_far(c_):
-        times_mix(sb, sb_mix, [(zs[4] * 8 + c_ * 4, 4)])
 
     kinds = {}
     sent = []
@@ -136,6 +108,34 @@
     def b_cols(z_, c_, first, size):
         return sb.at[pl.ds(z_ * 8 + c_ * 4 + first, size)]
 
+    def times_mix(*runs):
+        rows = jnp.concatenate([source[pl.ds(at, size)] for source, _, at, size in runs], axis=0)
+        rows = rows.reshape(-1, features)
+        for first in thirds:
+            block = jnp.dot(
+                rows, mix_w[:, pl.ds(first, 256)], preferred_element_type=jnp.float32
+            ).astype(jnp.bfloat16).reshape(-1, samples, 256)
+            done = 0
+            for _, result, at, size in runs:
+                result[pl.ds(at, size), :, pl.ds(first, 256)] = block[done : done + size]
+                done += size
+
+    def some_a(y_, half):
+        return [(sa, sa_mix, y_ * 16 + 2 * half + 4 * q, 2) for q in range(4)]
+
+    def some_b(z_, c_):
+        return [(sb, sb_mix, z_ * 8 + c_ * 4, 4)]
+
+    def own_b(d):
+        return some_b(zs[8 - d], core) + some_b(zs[d], core)
+
+    def products(z_, c_):
+        return sb_mix.at[pl.ds(z_ * 8 + c_ * 4, 4)]
+
+    def send_products(d):
+        for sign, z_ in (("+", zs[8 - d]), ("-", zs[d])):
+            send(f"m{sign}{d}", products(z_, core), products(z_, core), "c")
+
     def direct(y_, k):
         return a_cols(y_, 4 * lax.rem(x + k, 4) + 2, 2)
 
@@ -143,14 +143,14 @@
         return a_cols(y_, 4 * lax.rem(x + k, 4) + 3, 1)
 
     shared = a_cols(y, 4 * x, 2)
-    send("l+", plist.at[x, y], plist.at[x, y], "y+")
-    send("l-", plist.at[x, y], plist.at[x, y], "y-")
     for p in (0, 1):
         send(f"z+0{p}", b_cols(z, core, 2 * p, 2), b_cols(z, core, 2 * p, 2), "z+")
         send(f"z-0{p}", b_cols(z, core, 2 * (1 - p), 2), b_cols(z, core, 2 * (1 - p), 2), "z-")
         if p == 0:
             send("y+S", shared, shared, "y+")
             send("y-S", shared, shared, "y-")
+    send("l+", plist.at[x, y], plist.at[x, y], "y+")
+    send("l-", plist.at[x, y], plist.at[x, y], "y-")
     send("y+D0", direct(y, 0), direct(y, 0), "y+")
     send("y-D0", direct(y, 0), direct(y, 0), "y-")
     send("c0", b_cols(z, core, 0, 4), b_cols(z, core, 0, 4), "c")
@@ -178,15 +178,11 @@
             send(f"z-{d}{p}", down, down, "z-")
         send(f"c-{d}{p}", down, down, "c")
 
-    mix_a(y, 0, 1, 0)
-    mix_a(y, 0, 1, 1)
-    arrive_c0()
-    mix_b(0)
+    times_mix(*some_b(z, core), *some_a(y, 0))
+    times_mix(*some_a(y, 1))
+    send("m0", products(z, core), products(z, core), "c")
 
     below, above = a_cols(yl, 4 * x, 2), a_cols(yr, 4 * x, 2)
-    arrive("l+", plist.at[x, yl], "y-")
-    send("l+2", plist.at[x, yl], plist.at[x, yl], "y+")
-    arrive("l-", plist.at[x, yr], "y+")
     arrive("y+S", below, "y-")
     send("y+S2", below, below, "y+")
     send("x+b", below, below, "x+")
@@ -194,6 +190,9 @@
     arrive("y-S", above, "y+")
     send("x+a", above, above, "x+")
     send("x-a", above, above, "x-")
+    arrive("l+", plist.at[x, yl], "y-")
+    send("l+2", plist.at[x, yl], plist.at[x, yl], "y+")
+    arrive("l-", plist.at[x, yr], "y+")
     z_round(1, 0)
 
     arrive("y+D0", direct(yl, 0), "y-")
@@ -207,9 +206,7 @@
     arrive("l+2", plist.at[x, yo], "y-")
     send("lx+", plist.at[x], plist.at[x], "x+")
     send("lx-", plist.at[x], plist.at[x], "x-")
-    arrive_c(1, 0)
-    arrive_c(1, 1)
-    mix_b(1)
+    times_mix(*own_b(1))
 
     arrive("y+S2", a_cols(yo, 4 * x, 2), "y-")
     for j in (0, 1):
@@ -233,9 +230,8 @@
         send(to + "c", a_cols(yo, 4 * x + 2, 1), a_cols(yo, 4 * x + 2, 1), to)
     z_round(2, 1)
 
-    arrive_c(2, 0)
-    arrive_c(2, 1)
-    mix_b(2)
+    times_mix(*own_b(2))
+    send_products(1)
     early = len(sent)
     arrive("y-D2", direct(yr, 2), "y+")
     send("y-r2", last(yr, 2), last(yr, 2), "y-")
@@ -251,42 +247,47 @@
     arrive("x+a", a_cols(yr, 4 * xl, 2), "x-")
     arrive("x+b2", a_cols(yl, 4 * xo, 2), "x-")
     arrive("x-a2", a_cols(yr, 4 * xo, 2), "x+")
-    mix_a(yl, 2, 2, 0)
+    for far_y in (yl, yr):
+        times_mix(*some_a(far_y, 0))
+    send_products(2)
     got = a_cols(yo, 4 * xl + 2, 1)
     arrive("x+c", got, "x-")
     send("x+c2", got, got, "x+")
     z_round(3, 1)
     arrive("y-D3", direct(yr, 3), "y+")
     send("y-r3", last(yr, 3), last(yr, 3), "y-")
-    mix_a(yr, 0, 1, 1)
-    arrive_c(3, 0)
-    arrive_c(3, 1)
-    mix_b(3)
-    for k in (1, 2, 3):
-        arrive(f"y+D{k}", direct(yl, k), "y-")
-    mix_a(yl, 0, 1, 1)
-    arrive("x+f1", a_cols(yo, 4 * xl + 1, 1), "x-")
-    arrive("x-f0", a_cols(yo, 4 * xr, 1), "x+")
-    arrive("x+f02", a_cols(yo, 4 * xo, 1), "x-")
-    arrive("x-f12", a_cols(yo, 4 * xo + 1, 1), "x+")
-    mix_a(yo, 0, 1, 0)
-    arrive("lx-", plist.at[xr], "x+")
-    arrive("lx+2", plist.at[xo], "x-")
+    times_mix(*some_a(yr, 1), *own_b(3))
+    send_products(3)
     for copy in sent[:early]:
         copy.wait_send()
+    late = sent[early:]
 
     z_round(4, 0)
     arrive("x-c", a_cols(yo, 4 * xr + 2, 1), "x+")
     arrive("x+c2", a_cols(yo, 4 * xo + 2, 1), "x-")
     for k in range(4):
         arrive(f"y-r{k}", last(yo, k), "y+")
-    mix_a(yo, 0, 1, 1)
-    mix_far(core)
-    for copy in sent[early:-2]:
+    for k in (1, 2, 3):
+        arrive(f"y+D{k}", direct(yl, k), "y-")
+    arrive("x+f1", a_cols(yo, 4 * xl + 1, 1), "x-")
+    arrive("x-f0", a_cols(yo, 4 * xr, 1), "x+")
+    arrive("x+f02", a_cols(yo, 4 * xo, 1), "x-")
+    arrive("x-f12", a_cols(yo, 4 * xo + 1, 1), "x+")
+    times_mix(*some_a(yl, 1), *some_a(yo, 0), *some_a(yo, 1), *some_b(zs[4], core))
+    for copy in late:
         copy.wait_send()
+    arrive("lx-", plist.at[xr], "x+")
+    arrive("lx+2", plist.at[xo], "x-")
+    arrive_c0()
+    arrive("m0", products(z, other), "c")
+    for d in (1, 2, 3):
+        arrive_c(d, 0)
+        arrive_c(d, 1)
+        arrive(f"m+{d}", products(zs[8 - d], other), "c")
+        arrive(f"m-{d}", products(zs[d], other), "c")
     arrive_c(4, 0)
-    mix_far(other)
-    sent[:-2] = []
+    times_mix(*some_b(zs[4], other))
+    del sent[:-2]
     for copy in sent:
         copy.wait_send()
     assert len(kinds) <= COPIES
@@ -438,12 +439,16 @@
         for h in halves:
             raw[h] = scores(step, h)
 
-    def step_body(step, carry):
+    def one_step(step):
         now = [raw[h] for h in halves]
         pool(step - 1)
         for h in halves:
             keep_weights(now[h], h)
         keep_scores(jnp.minimum(step + 1, steps - 1))
+
+    def two_steps(turn, carry):
+        one_step(2 * turn + 1)
+        one_step(2 * turn + 2)
         return carry
 
     @pl.when(steps > 0)
@@ -452,7 +457,8 @@
         for h in halves:
             keep_weights(raw[h], h)
         keep_scores(jnp.minimum(1, steps - 1))
-        lax.fori_loop(1, steps, step_body, 0)
+        lax.fori_loop(0, (steps - 1) // 2, two_steps, 0)
+        pl.when(lax.rem(steps, 2) == 0)(lambda: one_step(steps - 1))
         pool(steps - 1)
 
     load.wait()

time: 65.4 us -> 65.4 us (level)
  the two profiles are of different devices: /device:TPU:1 before, /device:TPU:2 now
where the time goes in v4:
time: 65.4 us; the launch traced here: 65.6 us
  Pallas kernels  64.4 us (98%)
  between operations  0.68 us (1%)
    pallas_call x1, Pallas kernels, gather_blocks(): pl.pallas_call(gather_kernel, out_shape=(blocks,) * 4 + (pltpu.VMEM((4, 4...  47.3 us
    pallas_call x1, Pallas kernels, score_pairs(): pl.pallas_call(score_kernel, out_shape=pltpu.VMEM((8, 1, 128), jnp.float3...  8.71 us
    pallas_call x1, Pallas kernels, return_scores(): pl.pallas_call(return_kernel, out_shape=jax.ShapeDtypeStruct((1, 64), jnp...  8.39 us

profile of v4, /device:TPU:2, one launch (start us, length us, event | category | flops | bytes accessed | tf_op | source)
XLA Modules:
  0.0 65.6 jit_solution(8164398164163791436)
XLA Ops:
  0.7 47.3 %gather_blocks.1 = (bf16[64,64,768]{2,1,0:T(8,128)(2,1)S(1)}, bf16[64,64,768]{2,1,0:T(8,128)(2,1)S(1)}, bf16[64,64,768]{2,1,0:T(8,128)(2,1)S(1)}, bf16[64,64,768]{2,1,0:T(8,128)(2,1)S(1)}, s32[4,4,1,128]{3,2,1,0:T(1,128)S(1)}) custom-call(bf16[16,64,768]{2,1,0:T(8,128)(2,1)} %cells.1, bf16[768,768]{1,0:T(8,128)(2,1)} %w_cell.1, bf16[768,768]{1,0:T(8,128)(2,1)} %w_mix.1, ...), custom_call_target="tpu_custom_call" | custom-call | tf_op jit(solution)/shard_map/gather_blocks/pallas_call | solution.py:303
  48.0 8.7 %score_pairs.1.part = f32[8,1,128]{2,1,0:T(1,128)S(1)} custom-call(bf16[64,64,768]{2,1,0:T(8,128)(2,1)S(1)} %get-tuple-element.10.sa, bf16[64,64,768]{2,1,0:T(8,128)(2,1)S(1)} %get-tuple-element.11.sb, bf16[64,64,768]{2,1,0:T(8,128)(2,1)S(1)} %get-tuple-element.12.sa_mix, bf16[64,64,768]{2,1,0:T(8,128)(2,1)S(1)} %get-tuple-element.13.sb_mix, ...), custom_call_target="tpu_custom_call" | custom-call | tf_op jit(solution)/shard_map/score_pairs/pallas_call | solution.py:489
  56.7 8.4 %return_scores.1 = f32[1,64]{1,0:T(1,128)S(1)} custom-call(f32[8,1,128]{2,1,0:T(1,128)S(1)} %score_pairs.1.part), custom_call_target="tpu_custom_call" | custom-call | tf_op jit(solution)/shard_map/return_scores/pallas_call | solution.py:546
  65.1 0.5 copy.9

commit v5 on v4

--- a/solution.py
+++ b/solution.py
@@ -321,9 +321,22 @@
     )(cells, w_cell, w_mix, pairs, counts)
 
 
+def add_scores(vectors, row, pool_w, target, out):
+    right = jnp.dot(vectors, pool_w[...], preferred_element_type=jnp.float32)
+    left = pltpu.roll(right, 2, 0)
+    inner = jnp.mean(left * right, axis=-1, keepdims=True)
+    size = jnp.mean(right * right, axis=-1, keepdims=True) + EPSILON
+    norms = size * pltpu.roll(size, 2, 0)
+    score = inner / jnp.sqrt(norms) / SOFTMAX_WARMTH
+    number = row + lax.broadcasted_iota(jnp.int32, (256, 128), 0)
+    for k in range(8):
+        hit = target[pl.ds(k, 1)] == number
+        out[k] += jnp.sum(jnp.where(hit, score, 0.0), axis=0, keepdims=True)
+
+
 def score_kernel(
-    sa, sb, sa_mix, sb_mix, plist, w_pool, out,
-    pool_w, raw, blend, pooled, target, table, lst, sem, list_sem
+    sa, sb, sa_mix, sb_mix, plist, w_pool, out, head, target, pool_w,
+    raw, blend, pooled, table, lst, sem, list_sem
 ):
     samples, features = sa.shape[1:]
     scale = 1.0 / math.sqrt(features)
@@ -463,23 +476,14 @@
 
     load.wait()
     out[...] = jnp.zeros_like(out)
+    head[...] = pooled[pl.ds(0, 256)].astype(jnp.bfloat16)
 
     def finish(chunk, carry):
         row = pl.multiple_of(chunk * 256, 256)
-        vectors = pooled[pl.ds(row, 256)].astype(jnp.bfloat16)
-        right = jnp.dot(vectors, pool_w[...], preferred_element_type=jnp.float32)
-        left = pltpu.roll(right, 2, 0)
-        inner = jnp.mean(left * right, axis=-1, keepdims=True)
-        size = jnp.mean(right * right, axis=-1, keepdims=True) + EPSILON
-        norms = size * pltpu.roll(size, 2, 0)
-        score = inner / jnp.sqrt(norms) / SOFTMAX_WARMTH
-        number = row + lax.broadcasted_iota(jnp.int32, (256, 128), 0)
-        for k in range(8):
-            hit = target[pl.ds(k, 1)] == number
-            out[k] += jnp.sum(jnp.where(hit, score, 0.0), axis=0, keepdims=True)
+        add_scores(pooled[pl.ds(row, 256)].astype(jnp.bfloat16), row, pool_w, target, out)
         return carry
 
-    lax.fori_loop(0, (steps + 31) // 32, finish, 0)
+    lax.fori_loop(1, (steps + 31) // 32, finish, 0)
 
 
 def score_pairs(sa, sb, sa_mix, sb_mix, plist, w_pool):
@@ -488,15 +492,18 @@
     two = 2 * samples
     return pl.pallas_call(
         score_kernel,
-        out_shape=pltpu.VMEM((8, 1, 128), jnp.float32),
+        out_shape=(
+            pltpu.VMEM((8, 1, 128), jnp.float32),
+            pltpu.VMEM((256, features), jnp.bfloat16),
+            pltpu.VMEM((8, 128), jnp.int32),
+            pltpu.VMEM(w_pool.shape, jnp.bfloat16),
+        ),
         in_specs=[vmem] * 5 + [pl.BlockSpec(memory_space=pltpu.HBM)],
-        out_specs=vmem,
+        out_specs=(vmem,) * 4,
         scratch_shapes=[
-            pltpu.VMEM(w_pool.shape, jnp.bfloat16),
             pltpu.VMEM((GROUP // 2, two, two), jnp.float32),
             pltpu.VMEM((GROUP // 2, 2 * two, 2 * two), jnp.bfloat16),
             pltpu.VMEM((2 * CAPACITY, features), jnp.float32),
-            pltpu.VMEM((8, 128), jnp.int32),
             pltpu.VMEM((3, 1, CAPACITY), jnp.int32),
             pltpu.SMEM((3, 1, CAPACITY), jnp.int32),
             pltpu.SemaphoreType.DMA,
@@ -507,7 +514,7 @@
     )(sa, sb, sa_mix, sb_mix, plist, w_pool)
 
 
-def return_kernel(part, out, landed, send_sem, recv_sem):
+def return_kernel(rest, head, target, pool_w, out, part, landed, send_sem, recv_sem):
     x, y, z, core = place()
     me = z * 8 + y * 2 + core
 
@@ -520,6 +527,8 @@
         pl.semaphore_signal(
             barrier, inc=1, device_id=(tx, z * 8 + ty * 2 + core), device_id_type=MESH
         )
+    part[...] = rest[...]
+    add_scores(head[...], 0, pool_w, target, part)
     pl.semaphore_wait(barrier, 15)
     sent = []
     for k in range(1, 16):
@@ -541,30 +550,31 @@
         copy.wait_send()
 
 
-def return_scores(part):
+def return_scores(*parts):
     vmem = pl.BlockSpec(memory_space=pltpu.VMEM)
     return pl.pallas_call(
         return_kernel,
         out_shape=jax.ShapeDtypeStruct((1, 64), jnp.float32),
-        in_specs=[vmem],
+        in_specs=[vmem] * 4,
         out_specs=vmem,
         scratch_shapes=[
+            pltpu.VMEM((8, 1, 128), jnp.float32),
             pltpu.VMEM((16, 1, 128), jnp.float32),
             pltpu.SemaphoreType.DMA((16,)),
             pltpu.SemaphoreType.DMA((16,)),
         ],
         compiler_params=pltpu.CompilerParams(
-            collective_id=1, has_side_effects=True, vmem_limit_bytes=1 << 20
+            collective_id=1, has_side_effects=True, vmem_limit_bytes=8 << 20
         ),
         name="return_scores",
-    )(part)
+    )(*parts)
 
 
 def local(cells, w_cell, w_mix, w_pool, pairs, counts):
     in_place = lambda v: pltpu.with_memory_space_constraint(v, pltpu.HBM)
     cells, w_cell, w_mix, w_pool = map(in_place, (cells, w_cell, w_mix, w_pool))
     blocks = gather_blocks(cells, w_cell, w_mix, in_place(pairs.T), counts)
-    return return_scores(score_pairs(*blocks, w_pool)).reshape(pairs.shape[0])
+    return return_scores(*score_pairs(*blocks, w_pool)).reshape(pairs.shape[0])
 
 
 def solution(mesh):

time: 65.4 us -> 64.9 us (level); the launches traced: 65.6 us -> 64 us
  Pallas kernels: 64.4 us -> 62.8 us
    pallas_call x1, Pallas kernels: 8.71 us -> 7.39 us  [score_pairs(): pl.pallas_call(score_kernel, out_shape=(pltpu.VMEM((8, 1, 128), jnp.float...]
where the time goes in v5:
time: 64.9 us; the launch traced here: 64 us
  Pallas kernels  62.8 us (97%)
  between operations  0.68 us (1%)
    pallas_call x1, Pallas kernels, gather_blocks(): pl.pallas_call(gather_kernel, out_shape=(blocks,) * 4 + (pltpu.VMEM((4, 4...  47.3 us
    pallas_call x1, Pallas kernels, return_scores(): pl.pallas_call(return_kernel, out_shape=jax.ShapeDtypeStruct((1, 64), jnp...  8.13 us
    pallas_call x1, Pallas kernels, score_pairs(): pl.pallas_call(score_kernel, out_shape=(pltpu.VMEM((8, 1, 128), jnp.float...  7.39 us

profile of v5, /device:TPU:2, one launch (start us, length us, event | category | flops | bytes accessed | tf_op | source)
XLA Modules:
  0.0 64.0 jit_solution(11754523377294345196)
XLA Ops:
  0.7 47.3 %gather_blocks.1 = (bf16[64,64,768]{2,1,0:T(8,128)(2,1)S(1)}, bf16[64,64,768]{2,1,0:T(8,128)(2,1)S(1)}, bf16[64,64,768]{2,1,0:T(8,128)(2,1)S(1)}, bf16[64,64,768]{2,1,0:T(8,128)(2,1)S(1)}, s32[4,4,1,128]{3,2,1,0:T(1,128)S(1)}) custom-call(bf16[16,64,768]{2,1,0:T(8,128)(2,1)} %cells.1, bf16[768,768]{1,0:T(8,128)(2,1)} %w_cell.1, bf16[768,768]{1,0:T(8,128)(2,1)} %w_mix.1, ...), custom_call_target="tpu_custom_call" | custom-call | tf_op jit(solution)/shard_map/gather_blocks/pallas_call | solution.py:303
  47.9 7.4 %score_pairs.1 = (f32[8,1,128]{2,1,0:T(1,128)S(1)}, bf16[256,768]{1,0:T(8,128)(2,1)S(1)}, s32[8,128]{1,0:T(8,128)S(1)}, bf16[768,768]{1,0:T(8,128)(2,1)S(1)}) custom-call(bf16[64,64,768]{2,1,0:T(8,128)(2,1)S(1)} %get-tuple-element.14.sa, bf16[64,64,768]{2,1,0:T(8,128)(2,1)S(1)} %get-tuple-element.15.sb, bf16[64,64,768]{2,1,0:T(8,128)(2,1)S(1)} %get-tuple-element.16.sa_mix, ...), custom_call_target="tpu_custom_call" | custom-call | tf_op jit(solution)/shard_map/score_pairs/pallas_call | solution.py:493
  55.3 8.1 %return_scores.1 = f32[1,64]{1,0:T(1,128)S(1)} custom-call(f32[8,1,128]{2,1,0:T(1,128)S(1)} %get-tuple-element.19.rest, bf16[256,768]{1,0:T(8,128)(2,1)S(1)} %get-tuple-element.20.head, s32[8,128]{1,0:T(8,128)S(1)} %get-tuple-element.21.target, bf16[768,768]{1,0:T(8,128)(2,1)S(1)} %get-tuple-element.22.pool_w), custom_call_target="tpu_custom_call" | custom-call | tf_op jit(solution)/shard_map/return_scores/pallas_call | solution.py:555
  63.4 0.5 copy.9
